TPU v7x, 128 devices: a whole 4x4x4 slice. The times are simulated.
128 devices in a mesh: prompt: 8 (over y, z_hi), sample: 16 (over x, z_lo, core).
Axes of the slice: x: 4, y: 4, z: 4 (z_hi: 2, z_lo: 2; z = z_hi * 2 + z_lo), core: 2. Of those that a mesh axis runs over, the one named last changes fastest.
Arguments:
- queries: bfloat16 [8, 128, 4096], P('prompt', 'sample'), may hold values from -250 to 250
- prompt_cache: bfloat16 [8, 16, 2048, 2048], P('prompt', 'sample'), may hold values from -6 to 6
- owner: int32 [8], P('prompt'), may hold values from 0 to 15
- prompt_len: int32 [8], P('prompt'), may hold values from 512 to 2048
- suffix_cache: bfloat16 [8, 128, 256, 2048], P('prompt', 'sample'), may hold values from -6 to 6
- suffix_len: int32 [8, 128], P('prompt', 'sample'), may hold values from 1 to 256
- new_kv: bfloat16 [8, 128, 2048], P('prompt', 'sample'), may hold values from -6 to 6
- out_weight: bfloat16 [4096, 4096], P(None, 'sample'), may hold values from -0.09375 to 0.09375
Outputs:
- mixed: bfloat16 [8, 128, 4096], P('prompt', None, 'sample')
All inputs are finite; a program needn't handle non-finite values.
Results may differ from a plain program's by a relative error of at most 0.007.
Values may be sent and summed in bfloat16 or wider, within the bound.
No kernel may reach another device: no remote copies, remote signals or barrier semaphores. Data moves between devices by JAX's collectives and lax.ppermute only.
A program may use at most 192 MiB of HBM per device.

v0:
```python
import math

import jax
import jax.numpy as jnp
from jax import lax
from jax.sharding import PartitionSpec as P

H = 32
KVH = 8
HD = 128


def copy_for_each(x, axis):
    copies = jnp.broadcast_to(x, (lax.axis_size(axis), *x.shape))
    return lax.all_to_all(copies, axis, split_axis=0, concat_axis=0, tiled=True)


def joined_along(pieces, dim):
    pieces = jnp.moveaxis(pieces, 0, dim)
    lengths = pieces.shape
    return pieces.reshape(*lengths[:dim], lengths[dim] * lengths[dim + 1], *lengths[dim + 2 :])


def gather_directly(x, axis, dim):
    pieces = copy_for_each(x, axis)
    return joined_along(pieces, dim)


def in_blocks(x, dim, devices):
    before, after = (x.shape[:dim], x.shape[dim + 1 :])
    return jnp.moveaxis(x.reshape(*before, devices, -1, *after), dim, 0)


def summed_on_arrival(x, axis, dim):
    pieces = in_blocks(x, dim, lax.axis_size(axis))
    arrived = lax.all_to_all(pieces, axis, split_axis=0, concat_axis=0, tiled=True)
    return arrived.sum(axis=0)


def sent_together(arrays, axis, dim, along):
    widths = [math.prod(a.shape[along:]) for a in arrays]
    both = jnp.concatenate(
        [a.reshape(*a.shape[:along], w) for a, w in zip(arrays, widths)], axis=along
    )
    out = summed_on_arrival(both, axis, dim)
    pieces = jnp.split(out, [sum(widths[:k]) for k in range(1, len(widths))], axis=along)
    return tuple((b.reshape(*out.shape[:along], *a.shape[along:]) for a, b in zip(arrays, pieces)))


def prefix_part(queries, cache, length):
    count = queries.shape[0]
    positions = cache.shape[0]
    query = queries.reshape(count, KVH, H // KVH, HD)
    keys = cache[:, : KVH * HD].reshape(positions, KVH, HD)
    values = cache[:, KVH * HD :].reshape(positions, KVH, HD)
    scores = jnp.einsum("sgjd,tgd->sgjt", query, keys, preferred_element_type=jnp.float32) * HD ** (
        -0.5
    )
    valid = jnp.arange(positions, dtype=jnp.int32) < length
    scores = jnp.where(valid, scores, -1e30)
    top = jnp.max(scores, axis=-1)
    weights = jnp.exp(scores - top[..., None])
    total = jnp.sum(weights, axis=-1)
    output = jnp.einsum(
        "sgjt,tgd->sgjd", weights.astype(jnp.bfloat16), values, preferred_element_type=jnp.float32
    )
    return (output.reshape(count, H, HD), top.reshape(count, H), total.reshape(count, H))


def suffix_part(queries, cache, lengths, own):
    count = queries.shape[0]
    positions = cache.shape[1]
    query = queries.reshape(count, KVH, H // KVH, HD)
    keys = cache[:, :, : KVH * HD].reshape(count, positions, KVH, HD)
    values = cache[:, :, KVH * HD :].reshape(count, positions, KVH, HD)
    own_key = own[:, : KVH * HD].reshape(count, KVH, HD)
    own_value = own[:, KVH * HD :].astype(jnp.float32).reshape(count, KVH, HD)
    scores = jnp.einsum(
        "sgjd,stgd->sgjt", query, keys, preferred_element_type=jnp.float32
    ) * HD ** (-0.5)
    valid = jnp.arange(positions, dtype=jnp.int32)[None, :] < lengths[:, None]
    scores = jnp.where(valid[:, None, None, :], scores, -1e30)
    own_score = jnp.einsum(
        "sgjd,sgd->sgj", query, own_key, preferred_element_type=jnp.float32
    ) * HD ** (-0.5)
    top = jnp.maximum(jnp.max(scores, axis=-1), own_score)
    weights = jnp.exp(scores - top[..., None])
    own_weight = jnp.exp(own_score - top)
    total = jnp.sum(weights, axis=-1) + own_weight
    output = jnp.einsum(
        "sgjt,stgd->sgjd", weights.astype(jnp.bfloat16), values, preferred_element_type=jnp.float32
    )
    own_rounded = own_weight.astype(jnp.bfloat16).astype(jnp.float32)
    output = output + own_rounded[..., None] * own_value[:, :, None, :]
    return (output.reshape(count, H, HD), top.reshape(count, H), total.reshape(count, H))


def combine(prefix, suffix):
    out_pre, top_pre, total_pre = prefix
    out_suf, top_suf, total_suf = suffix
    top = jnp.maximum(top_pre, top_suf)
    factor_pre = jnp.exp(top_pre - top)
    factor_suf = jnp.exp(top_suf - top)
    numer = out_pre * factor_pre[..., None] + out_suf * factor_suf[..., None]
    denom = total_pre * factor_pre + total_suf * factor_suf
    attn = numer / denom[..., None]
    return attn.reshape(attn.shape[0], H * HD).astype(jnp.bfloat16)


def local(queries, prompt_cache, owner, prompt_len, suffix_cache, suffix_len, new_kv, out_weight):
    local_queries = queries[0]
    length = prompt_len[0]
    holder = owner[0]
    gathered = gather_directly(queries, "sample", 1)
    every = gathered.shape[1]

    def compute():
        return prefix_part(gathered[0], prompt_cache[0, 0], length)

    def nothing():
        return (
            jnp.zeros((every, H, HD), jnp.float32),
            jnp.zeros((every, H), jnp.float32),
            jnp.zeros((every, H), jnp.float32),
        )

    out_all, top_all, total_all = lax.cond(lax.axis_index("sample") == holder, compute, nothing)
    out_mine, top_mine, total_mine = sent_together(
        (out_all[None], top_all[None], total_all[None]), "sample", 1, 3
    )
    prefix = (out_mine[0], top_mine[0], total_mine[0])
    suffix = suffix_part(local_queries, suffix_cache[0], suffix_len[0], new_kv[0])
    attn = combine(prefix, suffix)[None]
    mixed = jnp.dot(
        gather_directly(attn, "sample", 1)[0], out_weight, preferred_element_type=jnp.float32
    )[None]
    return mixed.astype(jnp.bfloat16)


def solution(mesh):
    in_specs = (
        P("prompt", "sample", None),
        P("prompt", "sample", None, None),
        P("prompt"),
        P("prompt"),
        P("prompt", "sample", None, None),
        P("prompt", "sample"),
        P("prompt", "sample", None),
        P(None, "sample"),
    )
    out_specs = P("prompt", None, "sample")
    return jax.shard_map(local, mesh=mesh, in_specs=in_specs, out_specs=out_specs, check_vma=False)
```

profile of v0, /device:TPU:80, one launch (start us, length us, event | category | flops | bytes accessed | tf_op | source)
XLA Modules:
  0.0 196.3 jit_solution(16894303568877500474)
XLA Ops:
  0.0 0.0 copy-start
  0.0 2.1 %broadcast_in_dim.25 = bf16[16,1,8,4096]{3,2,1,0:T(8,128)(2,1)} broadcast(bf16[8,4096]{1,0:T(8,128)(2,1)} %bitcast.106), dimensions={2,3} | broadcast | bytes 1114112 | tf_op jit(solution)/shard_map/broadcast_in_dim | solution.py:14
  2.1 5.5 %all-to-all-start = ((bf16[16,1,8,4096]{3,2,1,0:T(8,128)(2,1)}), bf16[16,1,8,4096]{3,2,1,0:T(8,128)(2,1)S(1)}, u32[]{:S(2)}, u32[]{:S(2)}) async-start(bf16[16,1,8,4096]{3,2,1,0:T(8,128)(2,1)} %broadcast_in_dim.25), calls=%async_computation | async-start | bytes 2097152 | tf_op jit(solution)/shard_map/all_to_all | solution.py:15
  8.2 0.7 fusion.25
  8.9 0.0 copy-start.3
  8.9 11.5 %copy.96 = bf16[1,8,256,2048]{2,3,1,0:T(8,128)(2,1)} copy(bf16[1,8,256,2048]{3,2,1,0:T(8,128)(2,1)} %param.14) | data formatting | bytes 16777216 | tf_op args[4]
  20.4 0.0 copy-done.3
  20.4 0.2 fusion.21
  20.6 3.4 %all-to-all-done = bf16[16,1,8,4096]{3,2,1,0:T(8,128)(2,1)S(1)} async-done(((bf16[16,1,8,4096]{3,2,1,0:T(8,128)(2,1)}), bf16[16,1,8,4096]{3,2,1,0:T(8,128)(2,1)S(1)}, u32[]{:S(2)}, u32[]{:S(2)}) %all-to-all-start) | async-done | bytes 1048608 | tf_op jit(solution)/shard_map/all_to_all | solution.py:15
  24.0 4.7 %conditional.1 = (f32[16,1,8,32,128]{4,2,3,1,0:T(8,128)}, f32[16,1,8,32,1]{4,2,3,1,0:T(8,128)}, f32[16,1,8,32,1]{4,2,3,1,0:T(8,128)}) conditional(s32[]{:T(128)} %convert_element_type.25, () %tuple.19, (s32[1]{0:T(128)}, bf16[1,1,2048,2048]{3,2,1,0:T(8,128)(2,1)}, bf16[16,1,8,4096]{3,2,1,0:T(8,128)(2,1)S(1)}) %tuple.20), branch_computations={%region_0.0_spmd, %region_1.4_spmd} | conditional | flops 4387235840 | bytes 164831328 | solution.py:127
  24.0 1.6 concatenate.5.clone2
  25.5 1.6 concatenate.5.clone
  27.1 1.5 concatenate.4.clone
  28.6 5.6 %pad_maximum_fusion = f32[16,1,8,32,130]{4,2,3,1,0:T(8,128)} fusion(f32[16,1,8,32,1]{4,2,3,1,0:T(8,128)} %get-tuple-element.48, f32[16,1,8,32,1]{4,2,3,1,0:T(8,128)} %get-tuple-element.47, f32[16,1,8,32,128]{4,2,3,1,0:T(8,128)} %get-tuple-element.46), kind=kLoop, calls=%fused_computation.13 | loop fusion | flops 1064960 | bytes 4259840 | tf_op jit(solution)/shard_map/concatenate | solution.py:42
  34.2 0.0 copy-start.4
  34.2 76.5 %all-to-all-start.1 = ((f32[16,1,8,32,130]{4,2,3,1,0:T(8,128)}), f32[16,1,8,32,130]{4,2,3,1,0:T(8,128)}, u32[]{:S(2)}, u32[]{:S(2)}) async-start(f32[16,1,8,32,130]{4,2,3,1,0:T(8,128)} %pad_maximum_fusion), calls=%async_computation.1 | async-start | bytes 8388608 | tf_op jit(solution)/shard_map/all_to_all | solution.py:36
  110.7 0.0 copy-done.4
  110.7 0.1 iota_compare_fusion.1
  110.8 5.1 %fusion.33 = (bf16[8,256,1024]{1,2,0:T(8,128)(2,1)S(1)}, bf16[8,256,1024]{1,2,0:T(8,128)(2,1)}) fusion(bf16[8,256,2048]{1,2,0:T(8,128)(2,1)} %bitcast.97), kind=kLoop, calls=%fused_computation.49 | loop fusion | bytes 16777216 | tf_op jit(solution)/shard_map/slice | solution.py:74
  115.9 0.7 fusion.35
  116.6 0.1 copy.99
  116.7 0.1 copy.100
  116.8 0.3 fusion.13
  117.1 0.1 copy.107
  117.2 0.1 copy.108
  117.3 3.4 %convolution_add_fusion = f32[8,8,4,128]{3,2,1,0:T(4,128)S(1)} fusion(bf16[8,256,8,128]{1,3,2,0:T(8,128)(2,1)} %bitcast.101, f32[8,8,4,256]{3,2,1,0:T(4,128)S(1)} %get-tuple-element.65, f32[8,8,4]{2,1,0:T(8,128)S(1)} %multiply_maximum_fusion, f32[8,8,128]{2,1,0:T(8,128)S(1)} %copy.103, f32[8,8,4]{2,1,0:T(8,128)S(1)} %get-tuple-element.61), kind=kOutput, calls=%fused_computation.16 | convolution fusion | flops 16973824 | bytes 4622336 | tf_op jit(solution)/shard_map/sgjt,stgd->sgjd/dot_general | solution.py:90
  120.7 0.1 reshape.125
  120.8 43.5 %all-to-all-done.1 = f32[16,1,8,32,130]{4,2,3,1,0:T(8,128)} async-done(((f32[16,1,8,32,130]{4,2,3,1,0:T(8,128)}), f32[16,1,8,32,130]{4,2,3,1,0:T(8,128)}, u32[]{:S(2)}, u32[]{:S(2)}) %all-to-all-start.1) | async-done | bytes 2129952 | tf_op jit(solution)/shard_map/all_to_all | solution.py:36
  164.3 2.5 %reduce_sum.29 = f32[8,32,130]{2,0,1:T(8,128)S(1)} reduce(f32[16,1,8,32,130]{4,2,3,1,0:T(8,128)} %all-to-all-done.1, f32[]{:T(128)} %constant.5.clone.1), dimensions={0,1}, to_apply=%region_4.5 | reduce | flops 499200 | bytes 2263044 | tf_op jit(solution)/shard_map/reduce_sum | solution.py:37
  166.8 0.1 fusion.34
  166.9 0.1 copy.95
  167.0 0.1 copy.106
  167.1 0.1 copy.109
  167.2 0.1 copy.105
  167.3 0.1 copy.101
  167.4 0.2 fusion.20
  167.6 0.1 broadcast_in_dim.40
  167.7 27.6 %all_to_all.15 = bf16[16,1,8,4096]{3,2,1,0:T(8,128)(2,1)S(1)} all-to-all(bf16[16,1,8,4096]{3,2,1,0:T(8,128)(2,1)S(1)} %broadcast_in_dim.40), channel_id=1, replica_groups=mesh['prompt'=8,'sample'=16] {'sample'}, dimensions={0} | all-to-all | bytes 2097152 | tf_op jit(solution)/shard_map/all_to_all | solution.py:15
  195.2 0.0 copy-done
  195.2 1.1 fusion.11
  (4 shorter events, 0.0 us)
Async XLA Ops:
  0.0 195.2 %copy-start = (bf16[4096,256]{1,0:T(8,128)(2,1)S(1)}, bf16[4096,256]{1,0:T(8,128)(2,1)}, u32[]{:S(2)}) copy-start(bf16[4096,256]{1,0:T(8,128)(2,1)} %param.17) | copy-start | bytes 6291460
  2.1 21.9 %all-to-all-start = ((bf16[16,1,8,4096]{3,2,1,0:T(8,128)(2,1)}), bf16[16,1,8,4096]{3,2,1,0:T(8,128)(2,1)S(1)}, u32[]{:S(2)}, u32[]{:S(2)}) async-start(bf16[16,1,8,4096]{3,2,1,0:T(8,128)(2,1)} %broadcast_in_dim.25), calls=%async_computation | async-start | bytes 2097152 | tf_op jit(solution)/shard_map/all_to_all | solution.py:15
  8.9 11.5 %copy-start.3 = (bf16[1,8,4096]{2,1,0:T(8,128)(2,1)S(1)}, bf16[1,8,4096]{2,1,0:T(8,128)(2,1)}, u32[]{:S(2)}) copy-start(bf16[1,8,4096]{2,1,0:T(8,128)(2,1)} %param.10) | copy-start | bytes 196612
  34.2 76.5 %copy-start.4 = (s32[1,8]{1,0:T(1,128)S(1)}, s32[1,8]{1,0:T(1,128)}, u32[]{:S(2)}) copy-start(s32[1,8]{1,0:T(1,128)} %param.15) | copy-start | bytes 100
  34.2 130.1 %all-to-all-start.1 = ((f32[16,1,8,32,130]{4,2,3,1,0:T(8,128)}), f32[16,1,8,32,130]{4,2,3,1,0:T(8,128)}, u32[]{:S(2)}, u32[]{:S(2)}) async-start(f32[16,1,8,32,130]{4,2,3,1,0:T(8,128)} %pad_maximum_fusion), calls=%async_computation.1 | async-start | bytes 8388608 | tf_op jit(solution)/shard_map/all_to_all | solution.py:36
where the time goes:
time: 199 us; the launch traced here: 196 us
  starting transfers between devices  82 us (41%)
  waiting for transfers between devices  46.8 us (24%)
  blocking collectives  27.6 us (14%)
  local copies, waits for them, and re-layouts  24.4 us (12%)
  other arithmetic  9.37 us (5%)
  matrix products  5.43 us (3%)
    all_to_all x1, starting transfers between devices, summed_on_arrival(): lax.all_to_all(pieces, axis, split_axis=0, concat_axis=0, tiled=True)  76.5 us
    all_to_all x1, waiting for transfers between devices, summed_on_arrival(): lax.all_to_all(pieces, axis, split_axis=0, concat_axis=0, tiled=True)  43.5 us
    all_to_all x1, blocking collectives, copy_for_each(): return lax.all_to_all(copies, axis, split_axis=0, concat_axis=0, tiled=True)  27.6 us
    unnamed x7, local copies, waits for them, and re-layouts  11.5 us
    concatenate x1, other arithmetic, sent_together(): jnp.concatenate([a.reshape(*a.shape[:along], w) for a, w in zip(arrays, w...  5.56 us
    all_to_all x1, starting transfers between devices, copy_for_each(): return lax.all_to_all(copies, axis, split_axis=0, concat_axis=0, tiled=True)  5.46 us
    slice x1, local copies, waits for them, and re-layouts, suffix_part(): keys = cache[:, :, :KVH * HD].reshape(count, positions, KVH, HD)  5.05 us
    concatenate x3, local copies, waits for them, and re-layouts, sent_together(): jnp.concatenate([a.reshape(*a.shape[:along], w) for a, w in zip(arrays, w...  4.67 us
  transfers between devices with their start and end apart: 2, of which 2 were waited for; matrix products, arithmetic and copies ran while one was open for 11% of the time, Pallas kernels for 0%

commit v1 on v0

v1 whole, which is shorter than its diff:
```python
import functools

import jax
import jax.numpy as jnp
from jax import lax
from jax.experimental import pallas as pl
from jax.experimental.pallas import tpu as pltpu
from jax.sharding import Mesh
from jax.sharding import PartitionSpec as P

H = 32
KVH = 8
GRP = H // KVH
HD = 128
KW = KVH * HD
QW = H * HD
SCALE = HD**-0.5
LOG2E = 1.4426950408889634
EXP_SCALE = SCALE * LOG2E
STAT = 2 * HD

NT = (((1,), (1,)), ((), ()))
NN = (((1,), (0,)), ((), ()))


def dot(a, b, dims):
    return lax.dot_general(a, b, dims, preferred_element_type=jnp.float32)


def three_parts(x):
    hi = x.astype(jnp.bfloat16).astype(jnp.float32)
    rest = x - hi
    mid = rest.astype(jnp.bfloat16).astype(jnp.float32)
    low = rest - mid
    return (hi + pltpu.roll(mid, 32, 1) + pltpu.roll(low, 64, 1)).astype(jnp.bfloat16)


def from_parts(x):
    x = x.astype(jnp.float32)
    return (pltpu.roll(x, HD - 64, 1) + pltpu.roll(x, HD - 32, 1)) + x


def prefix_kernel(info, q_ref, own_ref, other_ref, out_ref, cache, sems):
    count = q_ref.shape[0]
    positions = cache.shape[0]
    active = info[0]
    length = info[2]

    def copies(src):
        return [
            pltpu.make_async_copy(
                src.at[:, pl.ds(k * 2 * HD, 2 * HD)],
                cache.at[:, pl.ds(k * 2 * HD, 2 * HD)],
                sems.at[k],
            )
            for k in range(KVH)
        ]

    order = [0, 4, 1, 5, 2, 6, 3, 7]

    @pl.when(active == 1)
    def _():
        cs = copies(own_ref)
        for k in order:
            cs[k].start()

    @pl.when(active == 2)
    def _():
        cs = copies(other_ref)
        for k in order:
            cs[k].start()

    @pl.when(active > 0)
    def _():
        waits = copies(own_ref)
        lane = lax.broadcasted_iota(jnp.int32, (count, HD), 1)
        pos = lax.broadcasted_iota(jnp.int32, (1, positions), 1)
        bias = jnp.where(pos < length, 0.0, -1e30).astype(jnp.float32)

        def head(g, stats):
            m_all, l_all = stats
            q = jnp.concatenate(
                [
                    q_ref[:, pl.ds(pl.multiple_of((g * GRP + j) * HD, HD), HD)]
                    for j in range(GRP)
                ],
                axis=0,
            )
            keys = cache[:, pl.ds(pl.multiple_of(g * HD, HD), HD)]
            values = cache[:, pl.ds(pl.multiple_of(KW + g * HD, HD), HD)]
            s = dot(q, keys, NT) + bias
            top = jnp.max(s, axis=1, keepdims=True)
            e = jnp.exp2((s - top) * EXP_SCALE)
            total = jnp.sum(e, axis=1, keepdims=True)
            o = dot(e.astype(jnp.bfloat16), values, NN)
            for j in range(GRP):
                rows = slice(j * count, (j + 1) * count)
                out_ref[:, pl.ds(pl.multiple_of((g * GRP + j) * HD, HD), HD)] = o[rows].astype(
                    out_ref.dtype
                )
                here = lane == g * GRP + j
                m_all = jnp.where(here, top[rows], m_all)
                l_all = jnp.where(here, total[rows], l_all)
            return m_all, l_all

        stats = (jnp.zeros((count, HD), jnp.float32), jnp.zeros((count, HD), jnp.float32))
        for pair in range(KVH // 2):
            waits[pair].wait()
            waits[pair + 4].wait()
            stats = lax.fori_loop(2 * pair, 2 * pair + 2, head, stats)
        out_ref[:, pl.ds(QW, HD)] = three_parts(stats[0])
        out_ref[:, pl.ds(QW + HD, HD)] = three_parts(stats[1])


def prefix_call(info, q, own, other):
    count = q.shape[0]
    positions = own.shape[0]
    return pl.pallas_call(
        prefix_kernel,
        out_shape=jax.ShapeDtypeStruct((count, QW + STAT), jnp.bfloat16),
        in_specs=[
            pl.BlockSpec(memory_space=pltpu.SMEM),
            pl.BlockSpec(memory_space=pltpu.VMEM),
            pl.BlockSpec(memory_space=pl.ANY),
            pl.BlockSpec(memory_space=pl.ANY),
        ],
        out_specs=pl.BlockSpec(memory_space=pltpu.VMEM),
        scratch_shapes=[
            pltpu.VMEM((positions, 2 * KW), jnp.bfloat16),
            pltpu.SemaphoreType.DMA((KVH,)),
        ],
        cost_estimate=pl.CostEstimate(
            flops=4 * count * H * positions * HD,
            bytes_accessed=4 * positions * KW,
            transcendentals=count * H * positions,
        ),
        name="prefix",
    )(info, q, own, other)


def suffix_kernel(lens, q_ref, kv_ref, new_ref, o_ref, m_ref, l_ref):
    step = pl.program_id(0)
    positions = kv_ref.shape[1]
    q = q_ref[0].astype(jnp.float32)
    group = lax.broadcasted_iota(jnp.int32, (H, HD), 0) // GRP
    spread = jnp.concatenate([jnp.where(group == g, q, 0.0) for g in range(KVH)], axis=1)
    new = new_ref[0].astype(jnp.float32)
    s = dot(spread.astype(jnp.bfloat16), kv_ref[0, :, :KW], NT)
    pos = lax.broadcasted_iota(jnp.int32, (1, positions), 1)
    s = jnp.where(pos < lens[step], s, -1e30)
    own = jnp.sum(spread * new[:, :KW], axis=1, keepdims=True)
    top = jnp.maximum(jnp.max(s, axis=1, keepdims=True), own)
    e = jnp.exp2((s - top) * EXP_SCALE)
    own_e = jnp.exp2((own - top) * EXP_SCALE)
    total = jnp.sum(e, axis=1, keepdims=True) + own_e
    o = dot(e.astype(jnp.bfloat16), kv_ref[0, :, KW:], NN)
    o = o + own_e.astype(jnp.bfloat16).astype(jnp.float32) * new[:, KW:]
    picked = o[:, :HD]
    for g in range(1, KVH):
        picked = jnp.where(group == g, o[:, g * HD : (g + 1) * HD], picked)
    top = jnp.broadcast_to(top, (H, HD))
    total = jnp.broadcast_to(total, (H, HD))
    here = lax.broadcasted_iota(jnp.int32, (o_ref.shape[0], HD), 0) == step
    for h in range(H):
        at = slice(h * HD, (h + 1) * HD)
        o_ref[:, at] = jnp.where(here, picked[h : h + 1], o_ref[:, at])
        m_ref[:, at] = jnp.where(here, top[h : h + 1], m_ref[:, at])
        l_ref[:, at] = jnp.where(here, total[h : h + 1], l_ref[:, at])


def suffix_call(lens, q, kv, new):
    count, positions = kv.shape[:2]
    whole = pl.BlockSpec((count, QW), lambda i, n: (0, 0))
    shape = jax.ShapeDtypeStruct((count, QW), jnp.float32)
    return pl.pallas_call(
        suffix_kernel,
        out_shape=(shape,) * 3,
        grid_spec=pltpu.PrefetchScalarGridSpec(
            num_scalar_prefetch=1,
            grid=(count,),
            in_specs=[
                pl.BlockSpec((1, H, HD), lambda i, n: (i, 0, 0)),
                pl.BlockSpec((1, positions, 2 * KW), lambda i, n: (i, 0, 0)),
                pl.BlockSpec((1, 1, 2 * KW), lambda i, n: (i, 0, 0)),
            ],
            out_specs=(whole,) * 3,
        ),
        compiler_params=pltpu.CompilerParams(dimension_semantics=("arbitrary",)),
        cost_estimate=pl.CostEstimate(
            flops=4 * count * H * positions * KW,
            bytes_accessed=4 * count * positions * KW,
            transcendentals=count * H * positions,
        ),
        name="suffix",
    )(lens, q, kv, new)


def combine_kernel(where, got_ref, o_ref, m_ref, l_ref, out_ref):
    src = where[0]
    m_pre = from_parts(got_ref[src, :, QW : QW + HD])
    l_pre = from_parts(got_ref[src, :, QW + HD :])
    count = m_pre.shape[0]
    for h in range(H):
        at = slice(h * HD, (h + 1) * HD)
        m_suf = m_ref[:, at]
        m_h = jnp.broadcast_to(m_pre[:, h : h + 1], (count, HD))
        l_h = jnp.broadcast_to(l_pre[:, h : h + 1], (count, HD))
        top = jnp.maximum(m_h, m_suf)
        f_pre = jnp.exp2((m_h - top) * EXP_SCALE)
        f_suf = jnp.exp2((m_suf - top) * EXP_SCALE)
        numer = got_ref[src, :, at].astype(jnp.float32) * f_pre + o_ref[:, at] * f_suf
        denom = l_h * f_pre + l_ref[:, at] * f_suf
        attn = (numer / denom).astype(jnp.bfloat16)
        for k in range(out_ref.shape[0]):
            out_ref[k, :, at] = attn


def combine_call(where, got, o, m, l):
    peers, count, _ = got.shape
    vmem = pl.BlockSpec(memory_space=pltpu.VMEM)
    return pl.pallas_call(
        combine_kernel,
        out_shape=jax.ShapeDtypeStruct((peers, count, QW), jnp.bfloat16),
        in_specs=[pl.BlockSpec(memory_space=pltpu.SMEM), vmem, vmem, vmem, vmem],
        out_specs=vmem,
        name="combine",
    )(where, got, o, m, l)


CHIP = ("x", "z")


def to_chips(x):
    return lax.all_to_all(x, CHIP, split_axis=0, concat_axis=0, tiled=True)


def partner(x):
    return lax.ppermute(x, "core", [(0, 1), (1, 0)])


def local(queries, prompt_cache, owner, prompt_len, suffix_cache, suffix_len, new_kv, out_weight):
    peers = lax.axis_size(CHIP)
    core = lax.axis_index("core")
    q = queries[0]
    count = q.shape[0]
    all_q = to_chips(jnp.broadcast_to(q, (peers, *q.shape))).reshape(peers * count, QW)
    own_cache = prompt_cache[0, 0]
    other_cache = partner(own_cache)
    other_weight = partner(out_weight)

    o_suf, m_suf, l_suf = suffix_call(
        suffix_len[0], q.reshape(count, H, HD), suffix_cache[0], new_kv[0][:, None, :]
    )

    chip = owner[0] // 2
    mine = lax.axis_index(CHIP) == chip
    active = jnp.where(mine, jnp.where(owner[0] % 2 == core, 1, 2), 0)
    info = jnp.stack([active, chip, prompt_len[0]]).astype(jnp.int32)
    sent = prefix_call(info, all_q, own_cache, other_cache)
    got = to_chips(sent.reshape(peers, count, QW + STAT))
    attn = combine_call(chip[None], got, o_suf, m_suf, l_suf)
    attn = to_chips(attn).reshape(peers * count, QW)

    theirs = jnp.dot(attn, other_weight, preferred_element_type=jnp.float32).astype(jnp.bfloat16)
    back = partner(theirs).reshape(peers, count, -1)
    ours = jnp.dot(attn, out_weight, preferred_element_type=jnp.float32).astype(jnp.bfloat16)
    ours = ours.reshape(peers, count, -1)
    first = core == 0
    mixed = jnp.stack([jnp.where(first, ours, back), jnp.where(first, back, ours)], axis=1)
    return mixed.reshape(1, 2 * peers * count, -1)


def solution(mesh):
    prompts = mesh.devices.shape[0]
    fine = Mesh(mesh.devices.reshape(prompts, 4, 2, 2), ("prompt", "x", "z", "core"))
    sample = ("x", "z", "core")
    in_specs = (
        P("prompt", sample, None),
        P("prompt", sample, None, None),
        P("prompt"),
        P("prompt"),
        P("prompt", sample, None, None),
        P("prompt", sample),
        P("prompt", sample, None),
        P(None, sample),
    )
    out_specs = P("prompt", None, sample)
    return jax.shard_map(local, mesh=fine, in_specs=in_specs, out_specs=out_specs, check_vma=False)
```

time: 199 us -> 68.4 us (0.34)
  starting transfers between devices: 82 us -> 15.3 us
  waiting for transfers between devices: 46.8 us -> 17.1 us
  blocking collectives: 27.6 us -> 0 us
  Pallas kernels: 0 us -> 25 us
  local copies, waits for them, and re-layouts: 24.4 us -> 5.21 us
  other arithmetic: 9.37 us -> 0.61 us
  matrix products: 5.43 us -> 2.53 us
    all_to_all x2 -> x3, starting transfers between devices: 82 us -> 14.7 us  [to_chips(): return lax.all_to_all(x, CHIP, split_axis=0, concat_axis=0, tiled=True)]
    all_to_all x2 -> x3, waiting for transfers between devices: 46.8 us -> 16.4 us  [to_chips(): return lax.all_to_all(x, CHIP, split_axis=0, concat_axis=0, tiled=True)]
    all_to_all x1 -> x0, blocking collectives: 27.6 us -> none  [copy_for_each(): return lax.all_to_all(copies, axis, split_axis=0, concat_axis=0, tiled=True)]
    pallas_call x0 -> x3, Pallas kernels: none -> 25 us  [the longest x1 13.1 us: prefix_call(): pl.pallas_call(prefix_kernel, out_shape=jax.ShapeDtypeStruct((count, QW +...]
    unnamed x7 -> x11, local copies, waits for them, and re-layouts: 11.5 us -> 2.24 us
    concatenate x1 -> x0, other arithmetic: 5.56 us -> none  [sent_together(): jnp.concatenate([a.reshape(*a.shape[:along], w) for a, w in zip(arrays, w...]
    slice x1 -> x0, local copies, waits for them, and re-layouts: 5.05 us -> none  [suffix_part(): keys = cache[:, :, :KVH * HD].reshape(count, positions, KVH, HD)]
    concatenate x3 -> x0, local copies, waits for them, and re-layouts: 4.67 us -> none  [sent_together(): jnp.concatenate([a.reshape(*a.shape[:along], w) for a, w in zip(arrays, w...]
  transfers between devices with their start and end apart: 2 -> 6, of which waited for: 2 -> 3; matrix products, arithmetic and copies ran while one was open for 11% -> 6% of each run, Pallas kernels for 0% -> 37%
where the time goes in v1:
time: 68.4 us; the launch traced here: 67.2 us
  Pallas kernels  25 us (37%)
  waiting for transfers between devices  17.1 us (25%)
  starting transfers between devices  15.3 us (22%)
  local copies, waits for them, and re-layouts  5.21 us (8%)
  matrix products  2.53 us (4%)
  between operations  1.41 us (2%)
    all_to_all x3, waiting for transfers between devices, to_chips(): return lax.all_to_all(x, CHIP, split_axis=0, concat_axis=0, tiled=True)  16.4 us
    all_to_all x3, starting transfers between devices, to_chips(): return lax.all_to_all(x, CHIP, split_axis=0, concat_axis=0, tiled=True)  14.7 us
    pallas_call x1, Pallas kernels, prefix_call(): pl.pallas_call(prefix_kernel, out_shape=jax.ShapeDtypeStruct((count, QW +...  13.1 us
    pallas_call x1, Pallas kernels, suffix_call(): pl.pallas_call(suffix_kernel, out_shape=(shape,) * 3, grid_spec=pltpu.Pre...  9.72 us
    pallas_call x1, Pallas kernels, combine_call(): pl.pallas_call(combine_kernel, out_shape=jax.ShapeDtypeStruct((peers, cou...  2.26 us
    unnamed x11, local copies, waits for them, and re-layouts  2.24 us
    dot_general x1, matrix products, local(): jnp.dot(attn, other_weight, preferred_element_type=jnp.float32)  2.06 us
    broadcast_in_dim x1, local copies, waits for them, and re-layouts, local(): jnp.broadcast_to(q, (peers, *q.shape))  1.67 us
  transfers between devices with their start and end apart: 6, of which 3 were waited for; matrix products, arithmetic and copies ran while one was open for 6% of the time, Pallas kernels for 37%

profile of v1, /device:TPU:80, one launch (start us, length us, event | category | flops | bytes accessed | tf_op | source)
XLA Modules:
  0.0 67.2 jit_solution(11259001379514728085)
XLA Ops:
  0.0 0.0 collective-permute-start
  0.0 0.5 collective-permute-start.1
  0.5 1.7 %broadcast_in_dim.7 = bf16[8,8,4096]{2,1,0:T(8,128)(2,1)} broadcast(bf16[8,4096]{1,0:T(8,128)(2,1)} %bitcast.37), dimensions={1,2} | broadcast | bytes 589824 | tf_op jit(solution)/shard_map/broadcast_in_dim | solution.py:246
  2.2 5.4 %all-to-all-start = ((bf16[8,8,4096]{2,1,0:T(8,128)(2,1)}), bf16[8,8,4096]{2,1,0:T(8,128)(2,1)S(1)}, u32[]{:S(2)}, u32[]{:S(2)}) async-start(bf16[8,8,4096]{2,1,0:T(8,128)(2,1)} %broadcast_in_dim.7), calls=%async_computation | async-start | bytes 1048576 | tf_op jit(solution)/shard_map/all_to_all | solution.py:234
  8.9 0.6 pad_add_fusion.info
  9.5 7.7 %all-to-all-done = bf16[8,8,4096]{2,1,0:T(8,128)(2,1)S(1)} async-done(((bf16[8,8,4096]{2,1,0:T(8,128)(2,1)}), bf16[8,8,4096]{2,1,0:T(8,128)(2,1)S(1)}, u32[]{:S(2)}, u32[]{:S(2)}) %all-to-all-start) | async-done | bytes 524320 | tf_op jit(solution)/shard_map/all_to_all | solution.py:234
  17.2 0.0 copy-start.1
  17.2 0.0 collective-permute-done.other_ref
  17.2 0.8 %copy-done.1 = bf16[8,8,4096]{2,1,0:T(8,128)(2,1)} copy-done((bf16[8,8,4096]{2,1,0:T(8,128)(2,1)}, bf16[8,8,4096]{2,1,0:T(8,128)(2,1)S(1)}, u32[]{:S(2)}) %copy-start.1) | copy-done | bytes 524312
  18.0 0.0 copy-start.3
  18.0 0.0 copy-start.4
  18.0 13.1 %prefix.1 = bf16[64,4352]{1,0:T(8,128)(2,1)} custom-call(s32[3]{0:T(128)} %pad_add_fusion.info, bf16[64,4096]{1,0:T(8,128)(2,1)} %bitcast.35, bf16[2048,2048]{1,0:T(8,128)(2,1)} %bitcast.32, bf16[2048,2048]{1,0:T(8,128)(2,1)} %collective-permute-done.other_ref), custom_call_target="tpu_custom_call" | custom-call | flops 2147483648 | bytes 8388608 | tf_op jit(solution)/shard_map/prefix/pallas_call | solution.py:118
  31.1 3.5 %all-to-all-start.1 = ((bf16[8,8,4352]{2,1,0:T(8,128)(2,1)}), bf16[8,8,4352]{2,1,0:T(8,128)(2,1)S(1)}, u32[]{:S(2)}, u32[]{:S(2)}) async-start(bf16[8,8,4352]{2,1,0:T(8,128)(2,1)} %bitcast.34), calls=%async_computation.1 | async-start | bytes 1114112 | tf_op jit(solution)/shard_map/all_to_all | solution.py:234
  34.6 0.0 copy-done.3
  34.6 0.6 copy.14
  35.3 0.0 copy-done.4
  35.3 0.7 copy.10.new_ref
  35.9 9.7 %suffix.1 = (f32[8,4096]{1,0:T(8,128)}, f32[8,4096]{1,0:T(8,128)}, f32[8,4096]{1,0:T(8,128)}) custom-call(s32[8]{0:T(128)} %bitcast.40, bf16[8,32,128]{2,1,0:T(8,128)(2,1)} %bitcast.36, bf16[8,256,2048]{2,1,0:T(8,128)(2,1)} %bitcast.33, bf16[8,1,2048]{2,1,0:T(2,128)(2,1)} %copy.10.new_ref), custom_call_target="tpu_custom_call" | custom-call | flops 268435456 | bytes 8388608 | tf_op jit(solution)/shard_map/suffix/pallas_call | solution.py:175
  45.7 0.0 all-to-all-done.1.got_ref
  45.7 0.0 copy-start
  45.7 0.8 %copy-done = bf16[8,8,4352]{2,1,0:T(8,128)(2,1)} copy-done((bf16[8,8,4352]{2,1,0:T(8,128)(2,1)}, bf16[8,8,4352]{2,1,0:T(8,128)(2,1)S(1)}, u32[]{:S(2)}) %copy-start) | copy-done | bytes 557080
  46.5 2.3 %combine.1 = bf16[8,8,4096]{2,1,0:T(8,128)(2,1)} custom-call(s32[1]{0:T(128)} %bitcast.1.where, bf16[8,8,4352]{2,1,0:T(8,128)(2,1)} %copy-done, f32[8,4096]{1,0:T(8,128)} %get-tuple-element.8.o_ref, f32[8,4096]{1,0:T(8,128)} %get-tuple-element.9.m_ref, f32[8,4096]{1,0:T(8,128)} %get-tuple-element.10.l_ref), custom_call_target="tpu_custom_call" | custom-call | tf_op jit(solution)/shard_map/combine/pallas_call | solution.py:221
  48.7 0.0 copy-start.2
  48.7 5.8 %all-to-all-start.2 = ((bf16[8,8,4096]{2,1,0:T(8,128)(2,1)}), bf16[8,8,4096]{2,1,0:T(8,128)(2,1)S(1)}, u32[]{:S(2)}, u32[]{:S(2)}) async-start(bf16[8,8,4096]{2,1,0:T(8,128)(2,1)} %combine.1), calls=%async_computation.2 | async-start | bytes 1048576 | tf_op jit(solution)/shard_map/all_to_all | solution.py:234
  54.5 0.0 collective-permute-done.1
  54.5 8.7 %all-to-all-done.2 = bf16[8,8,4096]{2,1,0:T(8,128)(2,1)S(1)} async-done(((bf16[8,8,4096]{2,1,0:T(8,128)(2,1)}), bf16[8,8,4096]{2,1,0:T(8,128)(2,1)S(1)}, u32[]{:S(2)}, u32[]{:S(2)}) %all-to-all-start.2) | async-done | bytes 524320 | tf_op jit(solution)/shard_map/all_to_all | solution.py:234
  63.2 2.1 %convolution_convert_fusion = bf16[64,256]{1,0:T(8,128)(2,1)S(1)} fusion(bf16[4096,256]{1,0:T(8,128)(2,1)} %collective-permute-done.1, bf16[8,8,4096]{2,1,0:T(8,128)(2,1)S(1)} %all-to-all-done.2), kind=kOutput, calls=%fused_computation | convolution fusion | flops 134234112 | bytes 2654208 | tf_op jit(solution)/shard_map/dot_general | solution.py:264
  65.2 0.1 collective-permute-start.2
  65.3 0.0 copy-done.2
  65.3 0.5 convolution_convert_fusion.1
  65.8 0.7 %collective-permute-done.2 = bf16[64,256]{1,0:T(8,128)(2,1)S(1)} collective-permute-done((bf16[64,256]{1,0:T(8,128)(2,1)S(1)}, bf16[64,256]{1,0:T(8,128)(2,1)S(1)}, u32[]{:S(2)}, u32[]{:S(2)}) %collective-permute-start.2) | collective-permute-done | bytes 32800 | tf_op jit(solution)/shard_map/ppermute | solution.py:238
  66.5 0.6 copy.11
  (2 shorter events, 0.0 us)
Async XLA Ops:
  0.0 17.2 %collective-permute-start = (bf16[2048,2048]{1,0:T(8,128)(2,1)}, bf16[2048,2048]{1,0:T(8,128)(2,1)}, u32[]{:S(2)}, u32[]{:S(2)}) collective-permute-start(bf16[2048,2048]{1,0:T(8,128)(2,1)} %bitcast.31), channel_id=1, source_target_pairs={{0,1},{1,0},{2,3},{3,2},{4,5},{5,4},{6,7},{7,6},{8,9},{9,8},{10,11... | collective-permute-start | bytes 25165832 | tf_op jit(solution)/shard_map/ppermute | solution.py:238
  0.0 54.5 %collective-permute-start.1 = (bf16[4096,256]{1,0:T(8,128)(2,1)}, bf16[4096,256]{1,0:T(8,128)(2,1)}, u32[]{:S(2)}, u32[]{:S(2)}) collective-permute-start(bf16[4096,256]{1,0:T(8,128)(2,1)} %param.15), channel_id=1, source_target_pairs={{0,1},{1,0},{2,3},{3,2},{4,5},{5,4},{6,7},{7,6},{8,9},{9,8},{10,11... | collective-permute-start | bytes 6291464 | tf_op jit(solution)/shard_map/ppermute | solution.py:238
  2.2 15.0 %all-to-all-start = ((bf16[8,8,4096]{2,1,0:T(8,128)(2,1)}), bf16[8,8,4096]{2,1,0:T(8,128)(2,1)S(1)}, u32[]{:S(2)}, u32[]{:S(2)}) async-start(bf16[8,8,4096]{2,1,0:T(8,128)(2,1)} %broadcast_in_dim.7), calls=%async_computation | async-start | bytes 1048576 | tf_op jit(solution)/shard_map/all_to_all | solution.py:234
  17.2 0.8 %copy-start.1 = (bf16[8,8,4096]{2,1,0:T(8,128)(2,1)}, bf16[8,8,4096]{2,1,0:T(8,128)(2,1)S(1)}, u32[]{:S(2)}) copy-start(bf16[8,8,4096]{2,1,0:T(8,128)(2,1)S(1)} %all-to-all-done) | copy-start | bytes 1572868
  18.0 16.6 %copy-start.3 = (bf16[1,8,4096]{2,1,0:T(8,128)(2,1)S(1)}, bf16[1,8,4096]{2,1,0:T(8,128)(2,1)}, u32[]{:S(2)}) copy-start(bf16[1,8,4096]{2,1,0:T(8,128)(2,1)} %param.8) | copy-start | bytes 196612
  18.0 17.3 %copy-start.4 = (bf16[1,8,2048]{2,1,0:T(8,128)(2,1)S(1)}, bf16[1,8,2048]{2,1,0:T(8,128)(2,1)}, u32[]{:S(2)}) copy-start(bf16[1,8,2048]{2,1,0:T(8,128)(2,1)} %param.14) | copy-start | bytes 98308
  31.1 14.6 %all-to-all-start.1 = ((bf16[8,8,4352]{2,1,0:T(8,128)(2,1)}), bf16[8,8,4352]{2,1,0:T(8,128)(2,1)S(1)}, u32[]{:S(2)}, u32[]{:S(2)}) async-start(bf16[8,8,4352]{2,1,0:T(8,128)(2,1)} %bitcast.34), calls=%async_computation.1 | async-start | bytes 1114112 | tf_op jit(solution)/shard_map/all_to_all | solution.py:234
  45.7 0.8 %copy-start = (bf16[8,8,4352]{2,1,0:T(8,128)(2,1)}, bf16[8,8,4352]{2,1,0:T(8,128)(2,1)S(1)}, u32[]{:S(2)}) copy-start(bf16[8,8,4352]{2,1,0:T(8,128)(2,1)S(1)} %all-to-all-done.1.got_ref) | copy-start | bytes 1671172
  48.7 16.6 %copy-start.2 = (bf16[4096,256]{1,0:T(8,128)(2,1)S(1)}, bf16[4096,256]{1,0:T(8,128)(2,1)}, u32[]{:S(2)}) copy-start(bf16[4096,256]{1,0:T(8,128)(2,1)} %param.15) | copy-start | bytes 6291460
  48.7 14.4 %all-to-all-start.2 = ((bf16[8,8,4096]{2,1,0:T(8,128)(2,1)}), bf16[8,8,4096]{2,1,0:T(8,128)(2,1)S(1)}, u32[]{:S(2)}, u32[]{:S(2)}) async-start(bf16[8,8,4096]{2,1,0:T(8,128)(2,1)} %combine.1), calls=%async_computation.2 | async-start | bytes 1048576 | tf_op jit(solution)/shard_map/all_to_all | solution.py:234
  65.2 1.3 %collective-permute-start.2 = (bf16[64,256]{1,0:T(8,128)(2,1)S(1)}, bf16[64,256]{1,0:T(8,128)(2,1)S(1)}, u32[]{:S(2)}, u32[]{:S(2)}) collective-permute-start(bf16[64,256]{1,0:T(8,128)(2,1)S(1)} %convolution_convert_fusion), channel_id=1, source_target_pairs={{0,1},{1,0},{2,3},{3,2},{4,5},{5,4},{6,7},{7,6},{8,9},{9,8},{10,11... | collective-permute-start | bytes 98312 | tf_op jit(solution)/shard_map/ppermute | solution.py:238

commit v2 on v1

v2 whole, which is shorter than its diff:
```python
import functools

import jax
import jax.numpy as jnp
from jax import lax
from jax.experimental import pallas as pl
from jax.experimental.pallas import tpu as pltpu
from jax.sharding import Mesh
from jax.sharding import PartitionSpec as P


H = 32
KVH = 8
GRP = H // KVH
HD = 128
KW = KVH * HD
QW = H * HD
SCALE = HD**-0.5
LOG2E = 1.4426950408889634
EXP_SCALE = SCALE * LOG2E
STAT = 2 * HD

NT = (((1,), (1,)), ((), ()))
NN = (((1,), (0,)), ((), ()))


def dot(a, b, dims):
    return lax.dot_general(a, b, dims, preferred_element_type=jnp.float32)


def three_parts(x):
    hi = x.astype(jnp.bfloat16).astype(jnp.float32)
    rest = x - hi
    mid = rest.astype(jnp.bfloat16).astype(jnp.float32)
    low = rest - mid
    return (hi + pltpu.roll(mid, 32, 1) + pltpu.roll(low, 64, 1)).astype(jnp.bfloat16)


def from_parts(x):
    x = x.astype(jnp.float32)
    return (pltpu.roll(x, HD - 64, 1) + pltpu.roll(x, HD - 32, 1)) + x


def prefix_kernel(info, q_ref, own_ref, other_ref, out_ref, cache, even, odd, sems):
    count = q_ref.shape[0]
    positions = cache.shape[0]
    active = info[0]
    length = info[2]
    pairs = KVH // 2

    def copies(src):
        cols = [pl.ds(k * 2 * HD, 2 * HD) for k in range(KVH)]
        return [
            pltpu.make_async_copy(src.at[:, at], cache.at[:, at], sems.at[k])
            for k, at in enumerate(cols)
        ]

    def start(src):
        cs = copies(src)
        for k in range(pairs):
            cs[k].start()
            cs[pairs + k].start()

    @pl.when(active == 1)
    def _():
        start(own_ref)

    @pl.when(active == 2)
    def _():
        start(other_ref)

    @pl.when(active > 0)
    def _():
        waits = copies(own_ref)
        lane = lax.broadcasted_iota(jnp.int32, (count, HD), 1)
        pos = lax.broadcasted_iota(jnp.int32, (1, positions), 1)
        bias = jnp.where(pos < length, 0.0, -1e30).astype(jnp.float32)
        first = lax.broadcasted_iota(jnp.int32, (positions, HD), 1) == 0
        ones = jnp.where(first, 1.0, 0.0).astype(jnp.bfloat16)
        held = (even, odd)

        def score(g):
            if g % 2 == 0:
                waits[g // 2].wait()
            if g % 2 == 0 and g:
                waits[pairs + g // 2].wait()
            q = [q_ref[:, h * HD : (h + 1) * HD] for h in range(g * GRP, (g + 1) * GRP)]
            s = dot(jnp.concatenate(q, axis=0), cache[:, g * HD : (g + 1) * HD], NT) + bias
            held[g % 2][...] = s
            return jnp.max(s, axis=1, keepdims=True)

        m_all = jnp.zeros((count, HD), jnp.float32)
        l_all = jnp.zeros((count, HD), jnp.float32)
        tops = [score(0)]
        waits[pairs].wait()
        for g in range(KVH):
            if g < KVH - 1:
                tops.append(score(g + 1))
            top = tops[g]
            e = jnp.exp2((held[g % 2][...] - top) * EXP_SCALE)
            values = cache[:, KW + g * HD : KW + (g + 1) * HD]
            o = dot(e.astype(jnp.bfloat16), jnp.concatenate([values, ones], axis=1), NN)
            for j in range(GRP):
                rows = slice(j * count, (j + 1) * count)
                h = g * GRP + j
                out_ref[:, h * HD : (h + 1) * HD] = o[rows, :HD].astype(out_ref.dtype)
                m_all = jnp.where(lane == h, top[rows], m_all)
                l_all = jnp.where(lane == h, o[rows, HD : HD + 1], l_all)
        out_ref[:, QW : QW + HD] = three_parts(m_all)
        out_ref[:, QW + HD :] = three_parts(l_all)


def prefix_call(info, q, own, other):
    count = q.shape[0]
    positions = own.shape[0]
    vmem = pl.BlockSpec(memory_space=pltpu.VMEM)
    raw = pl.BlockSpec(memory_space=pl.ANY)
    return pl.pallas_call(
        prefix_kernel,
        out_shape=jax.ShapeDtypeStruct((count, QW + STAT), jnp.bfloat16),
        in_specs=[pl.BlockSpec(memory_space=pltpu.SMEM), vmem, raw, raw],
        out_specs=vmem,
        scratch_shapes=[
            pltpu.VMEM((positions, 2 * KW), jnp.bfloat16),
            pltpu.VMEM((GRP * count, positions), jnp.float32),
            pltpu.VMEM((GRP * count, positions), jnp.float32),
            pltpu.SemaphoreType.DMA((KVH,)),
        ],
        compiler_params=pltpu.CompilerParams(vmem_limit_bytes=52 << 20),
        cost_estimate=pl.CostEstimate(
            flops=4 * count * H * positions * HD,
            bytes_accessed=4 * positions * KW,
            transcendentals=count * H * positions,
        ),
        name="prefix",
    )(info, q, own, other)


def suffix_kernel(base, lens, q_ref, new_ref, kv_ref, out_ref, kv, rows, sems):
    count, positions = kv.shape[:2]
    mine = range(base, base + count)
    copies = {
        i: pltpu.make_async_copy(kv_ref.at[i], kv.at[i - base], sems.at[i - base]) for i in mine
    }
    for i in mine:
        copies[i].start()
    q = q_ref[...].astype(jnp.float32)
    new = new_ref[...].astype(jnp.float32)
    group = lax.broadcasted_iota(jnp.int32, (H, HD), 0) // GRP
    pos = lax.broadcasted_iota(jnp.int32, (1, positions), 1)
    for i in mine:
        for h in range(H):
            rows[i - base, h : h + 1, :] = q[i : i + 1, h * HD : (h + 1) * HD]
    for i in mine:
        heads = rows[i - base]
        spread = jnp.concatenate([jnp.where(group == g, heads, 0.0) for g in range(KVH)], axis=1)
        own = jnp.sum(spread * new[i : i + 1, :KW], axis=1, keepdims=True)
        copies[i].wait()
        s = dot(spread.astype(jnp.bfloat16), kv[i - base, :, :KW], NT)
        s = jnp.where(pos < lens[i], s, -1e30)
        top = jnp.maximum(jnp.max(s, axis=1, keepdims=True), own)
        e = jnp.exp2((s - top) * EXP_SCALE)
        own_e = jnp.exp2((own - top) * EXP_SCALE)
        total = jnp.sum(e, axis=1, keepdims=True) + own_e
        o = dot(e.astype(jnp.bfloat16), kv[i - base, :, KW:], NN)
        o = o + own_e.astype(jnp.bfloat16).astype(jnp.float32) * new[i : i + 1, KW:]
        picked = o[:, :HD]
        for g in range(1, KVH):
            picked = jnp.where(group == g, o[:, g * HD : (g + 1) * HD], picked)
        top = jnp.broadcast_to(top, (H, HD))
        total = jnp.broadcast_to(total, (H, HD))
        for h in range(H):
            for k, part in enumerate((picked, top, total)):
                out_ref[i : i + 1, k * QW + h * HD : k * QW + (h + 1) * HD] = part[h : h + 1]


def suffix_call(base, count, limit, lens, q, new, kv):
    samples, positions, width = kv.shape
    vmem = pl.BlockSpec(memory_space=pltpu.VMEM)
    return pl.pallas_call(
        functools.partial(suffix_kernel, base),
        out_shape=jax.ShapeDtypeStruct((samples, 3 * QW), jnp.float32),
        in_specs=[
            pl.BlockSpec(memory_space=pltpu.SMEM),
            vmem,
            vmem,
            pl.BlockSpec(memory_space=pl.ANY),
        ],
        out_specs=vmem,
        scratch_shapes=[
            pltpu.VMEM((count, positions, width), kv.dtype),
            pltpu.VMEM((count, H, HD), jnp.float32),
            pltpu.SemaphoreType.DMA((count,)),
        ],
        compiler_params=pltpu.CompilerParams(vmem_limit_bytes=limit << 20),
        cost_estimate=pl.CostEstimate(
            flops=4 * count * H * positions * KW,
            bytes_accessed=4 * count * positions * KW,
            transcendentals=count * H * positions,
        ),
        name="suffix",
    )(lens, q, new, kv)


def copies_kernel(x_ref, out_ref, x, sem):
    pltpu.async_copy(x_ref, x, sem).wait()
    for k in range(out_ref.shape[0]):
        out_ref[k] = x[...]


def copies_call(x, peers):
    return pl.pallas_call(
        copies_kernel,
        out_shape=jax.ShapeDtypeStruct((peers, *x.shape), x.dtype),
        in_specs=[pl.BlockSpec(memory_space=pl.ANY)],
        out_specs=pl.BlockSpec(memory_space=pltpu.VMEM),
        scratch_shapes=[pltpu.VMEM(x.shape, x.dtype), pltpu.SemaphoreType.DMA],
        compiler_params=pltpu.CompilerParams(vmem_limit_bytes=4 << 20),
        name="copies",
    )(x)


def stage_kernel(x_ref, out_ref, sem):
    pltpu.async_copy(x_ref, out_ref, sem).wait()


def stage_call(x):
    return pl.pallas_call(
        stage_kernel,
        out_shape=jax.ShapeDtypeStruct(x.shape, x.dtype),
        in_specs=[pl.BlockSpec(memory_space=pl.ANY)],
        out_specs=pl.BlockSpec(memory_space=pltpu.VMEM),
        scratch_shapes=[pltpu.SemaphoreType.DMA],
        compiler_params=pltpu.CompilerParams(vmem_limit_bytes=4 << 20),
        cost_estimate=pl.CostEstimate(flops=0, bytes_accessed=2 * x.size, transcendentals=0),
        name="stage",
    )(x)


def combine_kernel(split, where, got_ref, early, late, out_ref, attn, outs):
    src = where[0]
    m_pre = from_parts(got_ref[src, :, QW : QW + HD])
    l_pre = from_parts(got_ref[src, :, QW + HD :])
    count = m_pre.shape[0]
    first = lax.broadcasted_iota(jnp.int32, (count, HD), 0) < split
    for h in range(H):
        at = slice(h * HD, (h + 1) * HD)
        cols = [slice(k * QW + h * HD, k * QW + (h + 1) * HD) for k in range(3)]
        o_suf, m_suf, l_suf = (jnp.where(first, early[:, c], late[:, c]) for c in cols)
        m_h = jnp.broadcast_to(m_pre[:, h : h + 1], (count, HD))
        l_h = jnp.broadcast_to(l_pre[:, h : h + 1], (count, HD))
        top = jnp.maximum(m_h, m_suf)
        f_pre = jnp.exp2((m_h - top) * EXP_SCALE)
        f_suf = jnp.exp2((m_suf - top) * EXP_SCALE)
        numer = got_ref[src, :, at].astype(jnp.float32) * f_pre + o_suf * f_suf
        denom = l_h * f_pre + l_suf * f_suf
        attn[:, at] = (numer / denom).astype(jnp.bfloat16)
    copies = [pltpu.make_async_copy(attn, out_ref.at[k], outs.at[k]) for k in range(out_ref.shape[0])]
    for c in copies:
        c.start()
    for c in copies:
        c.wait()


def combine_call(split, where, got, early, late):
    peers, count, _ = got.shape
    vmem = pl.BlockSpec(memory_space=pltpu.VMEM)
    return pl.pallas_call(
        functools.partial(combine_kernel, split),
        out_shape=jax.ShapeDtypeStruct((peers, count, QW), jnp.bfloat16),
        in_specs=[pl.BlockSpec(memory_space=pltpu.SMEM), vmem, vmem, vmem],
        out_specs=pl.BlockSpec(memory_space=pl.ANY),
        scratch_shapes=[pltpu.VMEM((count, QW), jnp.bfloat16), pltpu.SemaphoreType.DMA((peers,))],
        compiler_params=pltpu.CompilerParams(vmem_limit_bytes=8 << 20),
        name="combine",
    )(where, got, early, late)


def project(x, w):
    return jnp.dot(x, w, preferred_element_type=jnp.float32).astype(jnp.bfloat16)


def join_kernel(info, ours_ref, back_ref, out_ref):
    count = ours_ref.shape[1]
    ours, back = ours_ref[...], back_ref[...]
    first = info[0] == 0
    out_ref[:, :count] = jnp.where(first, ours, back)
    out_ref[:, count:] = jnp.where(first, back, ours)


def join_call(core, ours, back):
    peers, count, cols = ours.shape
    vmem = pl.BlockSpec(memory_space=pltpu.VMEM)
    return pl.pallas_call(
        join_kernel,
        out_shape=jax.ShapeDtypeStruct((peers, 2 * count, cols), ours.dtype),
        in_specs=[pl.BlockSpec(memory_space=pltpu.SMEM), vmem, vmem],
        out_specs=vmem,
        compiler_params=pltpu.CompilerParams(vmem_limit_bytes=4 << 20),
        name="join",
    )(core, ours, back)


CHIP = ("x", "z")


def to_chips(x):
    return lax.all_to_all(x, CHIP, split_axis=0, concat_axis=0, tiled=True)


def partner(x):
    return lax.ppermute(x, "core", [(0, 1), (1, 0)])


def local(queries, prompt_cache, owner, prompt_len, suffix_cache, suffix_len, new_kv, out_weight):
    peers = lax.axis_size(CHIP)
    core = lax.axis_index("core")
    q = queries[0]
    count = q.shape[0]
    split = 5
    own_cache = prompt_cache[0, 0]
    chip = owner[0] // 2
    mine = lax.axis_index(CHIP) == chip
    active = jnp.where(mine, jnp.where(owner[0] % 2 == core, 1, 2), 0)
    info = jnp.stack([active, chip, prompt_len[0]]).astype(jnp.int32)
    suffix_args = (suffix_len[0], q, new_kv[0], suffix_cache[0])
    other_cache = partner(own_cache)
    all_q = to_chips(copies_call(q, peers)).reshape(peers * count, QW)
    early = suffix_call(0, split, 57, *suffix_args)
    sent = prefix_call(info, all_q, own_cache, other_cache)
    got = to_chips(sent.reshape(peers, count, QW + STAT))
    late = suffix_call(split, count - split, 50, *suffix_args)
    attn = combine_call(split, chip[None], got, early, late)
    attn = to_chips(attn).reshape(peers * count, QW)
    other_weight = partner(out_weight)
    other_weight = stage_call(other_weight)
    theirs = project(attn, other_weight)
    back = partner(theirs).reshape(peers, count, -1)
    ours = project(attn, out_weight).reshape(peers, count, -1)
    mixed = join_call(core[None], ours, back)
    return mixed.reshape(1, 2 * peers * count, -1)


def solution(mesh):
    prompts = mesh.devices.shape[0]
    fine = Mesh(mesh.devices.reshape(prompts, 4, 2, 2), ("prompt", "x", "z", "core"))
    sample = ("x", "z", "core")
    in_specs = (
        P("prompt", sample, None),
        P("prompt", sample, None, None),
        P("prompt"),
        P("prompt"),
        P("prompt", sample, None, None),
        P("prompt", sample),
        P("prompt", sample, None),
        P(None, sample),
    )
    out_specs = P("prompt", None, sample)
    return jax.shard_map(local, mesh=fine, in_specs=in_specs, out_specs=out_specs, check_vma=False)
```

time: 68.4 us -> 60.8 us (0.89)
  the two profiles are of different devices: /device:TPU:80 before, /device:TPU:9 now
where the time goes in v2:
time: 60.8 us; the launch traced here: 60.2 us
  Pallas kernels  22.6 us (37%)
  starting transfers between devices  18 us (30%)
  waiting for transfers between devices  12.4 us (20%)
  local copies, waits for them, and re-layouts  4.76 us (8%)
  between operations  1.48 us (2%)
  matrix products  0.92 us (2%)
    all_to_all x3, starting transfers between devices, to_chips(): return lax.all_to_all(x, CHIP, split_axis=0, concat_axis=0, tiled=True)  14 us
    all_to_all x3, waiting for transfers between devices, to_chips(): return lax.all_to_all(x, CHIP, split_axis=0, concat_axis=0, tiled=True)  12 us
    pallas_call x2, Pallas kernels, suffix_call(): pl.pallas_call(functools.partial(suffix_kernel, base), out_shape=jax.Shap...  10.2 us
    pallas_call x1, Pallas kernels, prefix_call(): pl.pallas_call(prefix_kernel, out_shape=jax.ShapeDtypeStruct((count, QW +...  9.62 us
    unnamed x16, local copies, waits for them, and re-layouts  4.76 us
    ppermute x3, starting transfers between devices, partner(): return lax.ppermute(x, 'core', [(0, 1), (1, 0)])  3.96 us
  transfers between devices with their start and end apart: 6, of which 3 were waited for; matrix products, arithmetic and copies ran while one was open for 1% of the time, Pallas kernels for 37%

profile of v2, /device:TPU:9, one launch (start us, length us, event | category | flops | bytes accessed | tf_op | source)
XLA Modules:
  0.0 60.2 jit_solution(10631344197553039057)
XLA Ops:
  0.0 0.7 %collective-permute-start = (bf16[2048,2048]{1,0:T(8,128)(2,1)}, bf16[2048,2048]{1,0:T(8,128)(2,1)}, u32[]{:S(2)}, u32[]{:S(2)}) collective-permute-start(bf16[2048,2048]{1,0:T(8,128)(2,1)} %bitcast.37), channel_id=1, source_target_pairs={{0,1},{1,0},{2,3},{3,2},{4,5},{5,4},{6,7},{7,6},{8,9},{9,8},{10,11... | collective-permute-start | bytes 25165832 | tf_op jit(solution)/shard_map/ppermute | solution.py:312
  0.7 0.0 collective-permute-start.1
  0.7 0.0 copy-start.3
  0.7 0.8 %copy-done.3 = bf16[1,8,4096]{2,1,0:T(8,128)(2,1)S(1)} copy-done((bf16[1,8,4096]{2,1,0:T(8,128)(2,1)S(1)}, bf16[1,8,4096]{2,1,0:T(8,128)(2,1)}, u32[]{:S(2)}) %copy-start.3) | copy-done | bytes 65560
  1.5 0.9 %copies.1 = bf16[8,8,4096]{2,1,0:T(8,128)(2,1)} custom-call(bf16[8,4096]{1,0:T(8,128)(2,1)S(1)} %bitcast.28), custom_call_target="tpu_custom_call" | custom-call | tf_op jit(solution)/shard_map/copies/pallas_call | solution.py:212
  2.5 5.4 %all-to-all-start = ((bf16[8,8,4096]{2,1,0:T(8,128)(2,1)}), bf16[8,8,4096]{2,1,0:T(8,128)(2,1)S(1)}, u32[]{:S(2)}, u32[]{:S(2)}) async-start(bf16[8,8,4096]{2,1,0:T(8,128)(2,1)} %copies.1), calls=%async_computation | async-start | bytes 1048576 | tf_op jit(solution)/shard_map/all_to_all | solution.py:308
  9.2 0.1 pad_add_fusion.info
  9.3 7.7 %all-to-all-done = bf16[8,8,4096]{2,1,0:T(8,128)(2,1)S(1)} async-done(((bf16[8,8,4096]{2,1,0:T(8,128)(2,1)}), bf16[8,8,4096]{2,1,0:T(8,128)(2,1)S(1)}, u32[]{:S(2)}, u32[]{:S(2)}) %all-to-all-start) | async-done | bytes 524320 | tf_op jit(solution)/shard_map/all_to_all | solution.py:308
  16.9 0.0 collective-permute-done.other_ref
  16.9 0.0 copy-start.4
  16.9 0.0 copy-start.5
  16.9 0.0 copy-start.6
  16.9 9.6 %prefix.1 = bf16[64,4352]{1,0:T(8,128)(2,1)} custom-call(s32[3]{0:T(128)S(1)} %pad_add_fusion.info, bf16[64,4096]{1,0:T(8,128)(2,1)S(1)} %bitcast.26, bf16[2048,2048]{1,0:T(8,128)(2,1)} %bitcast.38, bf16[2048,2048]{1,0:T(8,128)(2,1)} %collective-permute-done.other_ref), custom_call_target="tpu_custom_call" | custom-call | flops 2147483648 | bytes 8388608 | tf_op jit(solution)/shard_map/prefix/pallas_call | solution.py:118
  26.6 3.5 %all-to-all-start.1 = ((bf16[8,8,4352]{2,1,0:T(8,128)(2,1)}), bf16[8,8,4352]{2,1,0:T(8,128)(2,1)S(1)}, u32[]{:S(2)}, u32[]{:S(2)}) async-start(bf16[8,8,4352]{2,1,0:T(8,128)(2,1)} %bitcast.7), calls=%async_computation.1 | async-start | bytes 1114112 | tf_op jit(solution)/shard_map/all_to_all | solution.py:308
  30.1 0.0 copy-done.4
  30.1 0.0 copy-done.5
  30.1 0.0 copy-done.6
  30.2 3.8 %suffix.3.late = f32[8,12288]{1,0:T(8,128)S(1)} custom-call(s32[8]{0:T(128)S(1)} %bitcast.34, bf16[8,4096]{1,0:T(8,128)(2,1)S(1)} %bitcast.29, bf16[8,2048]{1,0:T(8,128)(2,1)S(1)} %bitcast.31, bf16[8,256,2048]{2,1,0:T(8,128)(2,1)} %bitcast.35), custom_call_target="tpu_custom_call" | custom-call | flops 100663296 | bytes 3145728 | tf_op jit(solution)/shard_map/suffix/pallas_call | solution.py:180
  34.0 6.3 %suffix.2.early = f32[8,12288]{1,0:T(8,128)} custom-call(s32[8]{0:T(128)} %bitcast.33, bf16[8,4096]{1,0:T(8,128)(2,1)} %bitcast.27, bf16[8,2048]{1,0:T(8,128)(2,1)} %bitcast.30, bf16[8,256,2048]{2,1,0:T(8,128)(2,1)} %bitcast.36), custom_call_target="tpu_custom_call" | custom-call | flops 167772160 | bytes 5242880 | tf_op jit(solution)/shard_map/suffix/pallas_call | solution.py:180
  40.3 0.0 all-to-all-done.1.got_ref
  40.3 0.0 copy-start.2
  40.4 1.0 %copy-done.2 = f32[8,12288]{1,0:T(8,128)S(1)} copy-done((f32[8,12288]{1,0:T(8,128)S(1)}, f32[8,12288]{1,0:T(8,128)}, u32[]{:S(2)}) %copy-start.2) | copy-done | bytes 393240
  41.3 1.2 %combine.1 = bf16[8,8,4096]{2,1,0:T(8,128)(2,1)} custom-call(s32[1]{0:T(128)} %bitcast.2.where, bf16[8,8,4352]{2,1,0:T(8,128)(2,1)S(1)} %all-to-all-done.1.got_ref, f32[8,12288]{1,0:T(8,128)S(1)} %copy-done.2, f32[8,12288]{1,0:T(8,128)S(1)} %suffix.3.late), custom_call_target="tpu_custom_call" | custom-call | tf_op jit(solution)/shard_map/combine/pallas_call | solution.py:268
  42.5 5.1 %all-to-all-start.2 = ((bf16[8,8,4096]{2,1,0:T(8,128)(2,1)}), bf16[8,8,4096]{2,1,0:T(8,128)(2,1)S(1)}, u32[]{:S(2)}, u32[]{:S(2)}) async-start(bf16[8,8,4096]{2,1,0:T(8,128)(2,1)} %combine.1), calls=%async_computation.2 | async-start | bytes 1048576 | tf_op jit(solution)/shard_map/all_to_all | solution.py:308
  47.6 0.0 collective-permute-done.1.x_ref
  47.6 0.0 copy-start
  47.6 1.3 %copy-done = bf16[4096,256]{1,0:T(8,128)(2,1)} copy-done((bf16[4096,256]{1,0:T(8,128)(2,1)}, bf16[4096,256]{1,0:T(8,128)(2,1)S(1)}, u32[]{:S(2)}) %copy-start) | copy-done | bytes 2097176
  48.9 0.0 copy-start.1
  48.9 1.6 %copy-done.1 = bf16[4096,256]{1,0:T(8,128)(2,1)S(1)} copy-done((bf16[4096,256]{1,0:T(8,128)(2,1)S(1)}, bf16[4096,256]{1,0:T(8,128)(2,1)}, u32[]{:S(2)}) %copy-start.1) | copy-done | bytes 2097176
  50.5 0.1 stage.1
  50.7 4.3 %all-to-all-done.2 = bf16[8,8,4096]{2,1,0:T(8,128)(2,1)S(1)} async-done(((bf16[8,8,4096]{2,1,0:T(8,128)(2,1)}), bf16[8,8,4096]{2,1,0:T(8,128)(2,1)S(1)}, u32[]{:S(2)}, u32[]{:S(2)}) %all-to-all-start.2) | async-done | bytes 524320 | tf_op jit(solution)/shard_map/all_to_all | solution.py:308
  55.0 0.0 copy-start.7
  55.0 0.5 convolution_convert_fusion
  55.4 3.3 %collective-permute-start.2 = (bf16[64,256]{1,0:T(8,128)(2,1)S(1)}, bf16[64,256]{1,0:T(8,128)(2,1)S(1)}, u32[]{:S(2)}, u32[]{:S(2)}) collective-permute-start(bf16[64,256]{1,0:T(8,128)(2,1)S(1)} %convolution_convert_fusion), channel_id=1, source_target_pairs={{0,1},{1,0},{2,3},{3,2},{4,5},{5,4},{6,7},{7,6},{8,9},{9,8},{10,11... | collective-permute-start | bytes 98312 | tf_op jit(solution)/shard_map/ppermute | solution.py:312
  58.7 0.0 copy-done.7
  58.7 0.5 fusion.ours_ref
  59.2 0.4 collective-permute-done.2
  59.6 0.6 %join.1 = bf16[8,16,256]{2,1,0:T(8,128)(2,1)} custom-call(s32[1]{0:T(128)} %bitcast.info, bf16[8,8,256]{2,1,0:T(8,128)(2,1)S(1)} %fusion.ours_ref, bf16[8,8,256]{2,1,0:T(8,128)(2,1)S(1)} %bitcast.32), custom_call_target="tpu_custom_call" | custom-call | tf_op jit(solution)/shard_map/join/pallas_call | solution.py:294
Async XLA Ops:
  0.0 16.9 %collective-permute-start = (bf16[2048,2048]{1,0:T(8,128)(2,1)}, bf16[2048,2048]{1,0:T(8,128)(2,1)}, u32[]{:S(2)}, u32[]{:S(2)}) collective-permute-start(bf16[2048,2048]{1,0:T(8,128)(2,1)} %bitcast.37), channel_id=1, source_target_pairs={{0,1},{1,0},{2,3},{3,2},{4,5},{5,4},{6,7},{7,6},{8,9},{9,8},{10,11... | collective-permute-start | bytes 25165832 | tf_op jit(solution)/shard_map/ppermute | solution.py:312
  0.7 46.9 %collective-permute-start.1 = (bf16[4096,256]{1,0:T(8,128)(2,1)}, bf16[4096,256]{1,0:T(8,128)(2,1)S(1)}, u32[]{:S(2)}, u32[]{:S(2)}) collective-permute-start(bf16[4096,256]{1,0:T(8,128)(2,1)} %param.15), channel_id=1, source_target_pairs={{0,1},{1,0},{2,3},{3,2},{4,5},{5,4},{6,7},{7,6},{8,9},{9,8},{10,11... | collective-permute-start | bytes 6291464 | tf_op jit(solution)/shard_map/ppermute | solution.py:312
  0.7 0.8 %copy-start.3 = (bf16[1,8,4096]{2,1,0:T(8,128)(2,1)S(1)}, bf16[1,8,4096]{2,1,0:T(8,128)(2,1)}, u32[]{:S(2)}) copy-start(bf16[1,8,4096]{2,1,0:T(8,128)(2,1)} %param.8) | copy-start | bytes 196612
  2.5 14.5 %all-to-all-start = ((bf16[8,8,4096]{2,1,0:T(8,128)(2,1)}), bf16[8,8,4096]{2,1,0:T(8,128)(2,1)S(1)}, u32[]{:S(2)}, u32[]{:S(2)}) async-start(bf16[8,8,4096]{2,1,0:T(8,128)(2,1)} %copies.1), calls=%async_computation | async-start | bytes 1048576 | tf_op jit(solution)/shard_map/all_to_all | solution.py:308
  16.9 13.2 %copy-start.4 = (bf16[1,8,4096]{2,1,0:T(8,128)(2,1)S(1)}, bf16[1,8,4096]{2,1,0:T(8,128)(2,1)}, u32[]{:S(2)}) copy-start(bf16[1,8,4096]{2,1,0:T(8,128)(2,1)} %param.8) | copy-start | bytes 196612
  16.9 13.2 %copy-start.5 = (bf16[1,8,2048]{2,1,0:T(8,128)(2,1)S(1)}, bf16[1,8,2048]{2,1,0:T(8,128)(2,1)}, u32[]{:S(2)}) copy-start(bf16[1,8,2048]{2,1,0:T(8,128)(2,1)} %param.14) | copy-start | bytes 98308
  16.9 13.2 %copy-start.6 = (s32[1,8]{1,0:T(1,128)S(1)}, s32[1,8]{1,0:T(1,128)}, u32[]{:S(2)}) copy-start(s32[1,8]{1,0:T(1,128)} %param.13) | copy-start | bytes 100
  26.6 13.8 %all-to-all-start.1 = ((bf16[8,8,4352]{2,1,0:T(8,128)(2,1)}), bf16[8,8,4352]{2,1,0:T(8,128)(2,1)S(1)}, u32[]{:S(2)}, u32[]{:S(2)}) async-start(bf16[8,8,4352]{2,1,0:T(8,128)(2,1)} %bitcast.7), calls=%async_computation.1 | async-start | bytes 1114112 | tf_op jit(solution)/shard_map/all_to_all | solution.py:308
  40.3 1.0 %copy-start.2 = (f32[8,12288]{1,0:T(8,128)S(1)}, f32[8,12288]{1,0:T(8,128)}, u32[]{:S(2)}) copy-start(f32[8,12288]{1,0:T(8,128)} %suffix.2.early) | copy-start | bytes 1179652
  42.5 12.4 %all-to-all-start.2 = ((bf16[8,8,4096]{2,1,0:T(8,128)(2,1)}), bf16[8,8,4096]{2,1,0:T(8,128)(2,1)S(1)}, u32[]{:S(2)}, u32[]{:S(2)}) async-start(bf16[8,8,4096]{2,1,0:T(8,128)(2,1)} %combine.1), calls=%async_computation.2 | async-start | bytes 1048576 | tf_op jit(solution)/shard_map/all_to_all | solution.py:308
  47.6 1.3 %copy-start = (bf16[4096,256]{1,0:T(8,128)(2,1)}, bf16[4096,256]{1,0:T(8,128)(2,1)S(1)}, u32[]{:S(2)}) copy-start(bf16[4096,256]{1,0:T(8,128)(2,1)S(1)} %collective-permute-done.1.x_ref) | copy-start | bytes 6291460
  48.9 1.6 %copy-start.1 = (bf16[4096,256]{1,0:T(8,128)(2,1)S(1)}, bf16[4096,256]{1,0:T(8,128)(2,1)}, u32[]{:S(2)}) copy-start(bf16[4096,256]{1,0:T(8,128)(2,1)} %copy-done) | copy-start | bytes 6291460
  55.0 3.8 %copy-start.7 = (bf16[4096,256]{1,0:T(8,128)(2,1)S(1)}, bf16[4096,256]{1,0:T(8,128)(2,1)}, u32[]{:S(2)}) copy-start(bf16[4096,256]{1,0:T(8,128)(2,1)} %param.15) | copy-start | bytes 6291460
  55.4 4.1 %collective-permute-start.2 = (bf16[64,256]{1,0:T(8,128)(2,1)S(1)}, bf16[64,256]{1,0:T(8,128)(2,1)S(1)}, u32[]{:S(2)}, u32[]{:S(2)}) collective-permute-start(bf16[64,256]{1,0:T(8,128)(2,1)S(1)} %convolution_convert_fusion), channel_id=1, source_target_pairs={{0,1},{1,0},{2,3},{3,2},{4,5},{5,4},{6,7},{7,6},{8,9},{9,8},{10,11... | collective-permute-start | bytes 98312 | tf_op jit(solution)/shard_map/ppermute | solution.py:312

commit v3 on v2

--- a/solution.py
+++ b/solution.py
@@ -18,6 +18,7 @@
 SCALE = HD**-0.5
 LOG2E = 1.4426950408889634
 EXP_SCALE = SCALE * LOG2E
+GROUPS = (1, 3, 8)
 STAT = 2 * HD
 
 NT = (((1,), (1,)), ((), ()))
@@ -46,20 +47,20 @@
     positions = cache.shape[0]
     active = info[0]
     length = info[2]
-    pairs = KVH // 2
+    ends = GROUPS
 
     def copies(src):
-        cols = [pl.ds(k * 2 * HD, 2 * HD) for k in range(KVH)]
-        return [
-            pltpu.make_async_copy(src.at[:, at], cache.at[:, at], sems.at[k])
-            for k, at in enumerate(cols)
-        ]
+        found = []
+        for k, (lo, hi) in enumerate(zip((0, *ends[:-1]), ends)):
+            for part in range(2):
+                at = pl.ds(part * KW + lo * HD, (hi - lo) * HD)
+                sem = sems.at[2 * k + part]
+                found.append(pltpu.make_async_copy(src.at[:, at], cache.at[:, at], sem))
+        return found
 
     def start(src):
-        cs = copies(src)
-        for k in range(pairs):
-            cs[k].start()
-            cs[pairs + k].start()
+        for c in copies(src):
+            c.start()
 
     @pl.when(active == 1)
     def _():
@@ -80,10 +81,10 @@
         held = (even, odd)
 
         def score(g):
-            if g % 2 == 0:
-                waits[g // 2].wait()
-            if g % 2 == 0 and g:
-                waits[pairs + g // 2].wait()
+            if g == 0 or g in ends:
+                k = 0 if g == 0 else ends.index(g) + 1
+                waits[2 * k].wait()
+                waits[2 * k + 1].wait()
             q = [q_ref[:, h * HD : (h + 1) * HD] for h in range(g * GRP, (g + 1) * GRP)]
             s = dot(jnp.concatenate(q, axis=0), cache[:, g * HD : (g + 1) * HD], NT) + bias
             held[g % 2][...] = s
@@ -92,7 +93,6 @@
         m_all = jnp.zeros((count, HD), jnp.float32)
         l_all = jnp.zeros((count, HD), jnp.float32)
         tops = [score(0)]
-        waits[pairs].wait()
         for g in range(KVH):
             if g < KVH - 1:
                 tops.append(score(g + 1))
@@ -124,7 +124,7 @@
             pltpu.VMEM((positions, 2 * KW), jnp.bfloat16),
             pltpu.VMEM((GRP * count, positions), jnp.float32),
             pltpu.VMEM((GRP * count, positions), jnp.float32),
-            pltpu.SemaphoreType.DMA((KVH,)),
+            pltpu.SemaphoreType.DMA((2 * len(GROUPS),)),
         ],
         compiler_params=pltpu.CompilerParams(vmem_limit_bytes=52 << 20),
         cost_estimate=pl.CostEstimate(
@@ -202,24 +202,6 @@
     )(lens, q, new, kv)
 
 
-def copies_kernel(x_ref, out_ref, x, sem):
-    pltpu.async_copy(x_ref, x, sem).wait()
-    for k in range(out_ref.shape[0]):
-        out_ref[k] = x[...]
-
-
-def copies_call(x, peers):
-    return pl.pallas_call(
-        copies_kernel,
-        out_shape=jax.ShapeDtypeStruct((peers, *x.shape), x.dtype),
-        in_specs=[pl.BlockSpec(memory_space=pl.ANY)],
-        out_specs=pl.BlockSpec(memory_space=pltpu.VMEM),
-        scratch_shapes=[pltpu.VMEM(x.shape, x.dtype), pltpu.SemaphoreType.DMA],
-        compiler_params=pltpu.CompilerParams(vmem_limit_bytes=4 << 20),
-        name="copies",
-    )(x)
-
-
 def stage_kernel(x_ref, out_ref, sem):
     pltpu.async_copy(x_ref, out_ref, sem).wait()
 
@@ -317,7 +299,7 @@
     core = lax.axis_index("core")
     q = queries[0]
     count = q.shape[0]
-    split = 5
+    split = 4
     own_cache = prompt_cache[0, 0]
     chip = owner[0] // 2
     mine = lax.axis_index(CHIP) == chip
@@ -325,7 +307,8 @@
     info = jnp.stack([active, chip, prompt_len[0]]).astype(jnp.int32)
     suffix_args = (suffix_len[0], q, new_kv[0], suffix_cache[0])
     other_cache = partner(own_cache)
-    all_q = to_chips(copies_call(q, peers)).reshape(peers * count, QW)
+    q_copies = jnp.broadcast_to(q, (peers, *q.shape))
+    all_q = to_chips(q_copies).reshape(peers * count, QW)
     early = suffix_call(0, split, 57, *suffix_args)
     sent = prefix_call(info, all_q, own_cache, other_cache)
     got = to_chips(sent.reshape(peers, count, QW + STAT))

time: 60.8 us -> 59.4 us (0.977)
  Pallas kernels: 22.6 us -> 21.4 us
    unnamed x16 -> x14, local copies, waits for them, and re-layouts: 4.76 us -> 2.95 us
    broadcast_in_dim x0 -> x1, local copies, waits for them, and re-layouts: none -> 1.71 us  [local(): q_copies = jnp.broadcast_to(q, (peers, *q.shape))]
    pallas_call x1 -> x0, Pallas kernels: 0.93 us -> none  [copies_call(): pl.pallas_call(copies_kernel, out_shape=jax.ShapeDtypeStruct((peers, *x.s...]
  transfers between devices with their start and end apart: 6 -> 6, of which waited for: 3 -> 3; matrix products, arithmetic and copies ran while one was open for 1% -> 4% of each run, Pallas kernels for 37% -> 35%
where the time goes in v3:
time: 59.4 us; the launch traced here: 58.9 us
  Pallas kernels  21.4 us (36%)
  starting transfers between devices  17.7 us (30%)
  waiting for transfers between devices  12.7 us (21%)
  local copies, waits for them, and re-layouts  4.65 us (8%)
  between operations  1.49 us (3%)
  matrix products  0.92 us (2%)
    all_to_all x3, starting transfers between devices, to_chips(): return lax.all_to_all(x, CHIP, split_axis=0, concat_axis=0, tiled=True)  14 us
    all_to_all x3, waiting for transfers between devices, to_chips(): return lax.all_to_all(x, CHIP, split_axis=0, concat_axis=0, tiled=True)  12.3 us
    pallas_call x2, Pallas kernels, suffix_call(): pl.pallas_call(functools.partial(suffix_kernel, base), out_shape=jax.Shap...  10.3 us
    pallas_call x1, Pallas kernels, prefix_call(): pl.pallas_call(prefix_kernel, out_shape=jax.ShapeDtypeStruct((count, QW +...  9.15 us
    ppermute x3, starting transfers between devices, partner(): return lax.ppermute(x, 'core', [(0, 1), (1, 0)])  3.66 us
    unnamed x14, local copies, waits for them, and re-layouts  2.95 us
    broadcast_in_dim x1, local copies, waits for them, and re-layouts, local(): q_copies = jnp.broadcast_to(q, (peers, *q.shape))  1.71 us
  transfers between devices with their start and end apart: 6, of which 3 were waited for; matrix products, arithmetic and copies ran while one was open for 4% of the time, Pallas kernels for 35%

profile of v3, /device:TPU:9, one launch (start us, length us, event | category | flops | bytes accessed | tf_op | source)
XLA Modules:
  0.0 58.9 jit_solution(3169685607787800766)
XLA Ops:
  0.0 0.7 %collective-permute-start = (bf16[2048,2048]{1,0:T(8,128)(2,1)}, bf16[2048,2048]{1,0:T(8,128)(2,1)}, u32[]{:S(2)}, u32[]{:S(2)}) collective-permute-start(bf16[2048,2048]{1,0:T(8,128)(2,1)} %bitcast.37), channel_id=1, source_target_pairs={{0,1},{1,0},{2,3},{3,2},{4,5},{5,4},{6,7},{7,6},{8,9},{9,8},{10,11... | collective-permute-start | bytes 25165832 | tf_op jit(solution)/shard_map/ppermute | solution.py:294
  0.7 0.0 collective-permute-start.1
  0.7 1.7 %broadcast_in_dim.11 = bf16[8,8,4096]{2,1,0:T(8,128)(2,1)} broadcast(bf16[8,4096]{1,0:T(8,128)(2,1)} %bitcast.27), dimensions={1,2} | broadcast | bytes 589824 | tf_op jit(solution)/shard_map/broadcast_in_dim | solution.py:310
  2.4 5.4 %all-to-all-start = ((bf16[8,8,4096]{2,1,0:T(8,128)(2,1)}), bf16[8,8,4096]{2,1,0:T(8,128)(2,1)S(1)}, u32[]{:S(2)}, u32[]{:S(2)}) async-start(bf16[8,8,4096]{2,1,0:T(8,128)(2,1)} %broadcast_in_dim.11), calls=%async_computation | async-start | bytes 1048576 | tf_op jit(solution)/shard_map/all_to_all | solution.py:290
  9.1 0.1 pad_add_fusion.info
  9.2 7.7 %all-to-all-done = bf16[8,8,4096]{2,1,0:T(8,128)(2,1)S(1)} async-done(((bf16[8,8,4096]{2,1,0:T(8,128)(2,1)}), bf16[8,8,4096]{2,1,0:T(8,128)(2,1)S(1)}, u32[]{:S(2)}, u32[]{:S(2)}) %all-to-all-start) | async-done | bytes 524320 | tf_op jit(solution)/shard_map/all_to_all | solution.py:290
  16.9 0.0 collective-permute-done.other_ref
  16.9 9.1 %prefix.1 = bf16[64,4352]{1,0:T(8,128)(2,1)} custom-call(s32[3]{0:T(128)S(1)} %pad_add_fusion.info, bf16[64,4096]{1,0:T(8,128)(2,1)S(1)} %bitcast.26, bf16[2048,2048]{1,0:T(8,128)(2,1)} %bitcast.38, bf16[2048,2048]{1,0:T(8,128)(2,1)} %collective-permute-done.other_ref), custom_call_target="tpu_custom_call" | custom-call | flops 2147483648 | bytes 8388608 | tf_op jit(solution)/shard_map/prefix/pallas_call | solution.py:118
  26.0 3.5 %all-to-all-start.1 = ((bf16[8,8,4352]{2,1,0:T(8,128)(2,1)}), bf16[8,8,4352]{2,1,0:T(8,128)(2,1)S(1)}, u32[]{:S(2)}, u32[]{:S(2)}) async-start(bf16[8,8,4352]{2,1,0:T(8,128)(2,1)} %bitcast.7), calls=%async_computation.1 | async-start | bytes 1114112 | tf_op jit(solution)/shard_map/all_to_all | solution.py:290
  29.6 0.0 copy-start.3
  29.6 0.0 copy-start.4
  29.6 0.0 copy-start.5
  29.6 5.7 %suffix.2.early = f32[8,12288]{1,0:T(8,128)} custom-call(s32[8]{0:T(128)} %bitcast.33, bf16[8,4096]{1,0:T(8,128)(2,1)} %bitcast.28, bf16[8,2048]{1,0:T(8,128)(2,1)} %bitcast.30, bf16[8,256,2048]{2,1,0:T(8,128)(2,1)} %bitcast.35), custom_call_target="tpu_custom_call" | custom-call | flops 134217728 | bytes 4194304 | tf_op jit(solution)/shard_map/suffix/pallas_call | solution.py:180
  35.3 0.0 copy-done.3
  35.3 0.0 copy-done.4
  35.3 0.0 copy-done.5
  35.4 0.0 copy-start.2
  35.4 4.6 %suffix.3.late = f32[8,12288]{1,0:T(8,128)S(1)} custom-call(s32[8]{0:T(128)S(1)} %bitcast.34, bf16[8,4096]{1,0:T(8,128)(2,1)S(1)} %bitcast.29, bf16[8,2048]{1,0:T(8,128)(2,1)S(1)} %bitcast.31, bf16[8,256,2048]{2,1,0:T(8,128)(2,1)} %bitcast.36), custom_call_target="tpu_custom_call" | custom-call | flops 134217728 | bytes 4194304 | tf_op jit(solution)/shard_map/suffix/pallas_call | solution.py:180
  40.0 0.0 all-to-all-done.1.got_ref
  40.0 0.0 copy-done.2
  40.0 1.1 %combine.1 = bf16[8,8,4096]{2,1,0:T(8,128)(2,1)} custom-call(s32[1]{0:T(128)} %bitcast.2.where, bf16[8,8,4352]{2,1,0:T(8,128)(2,1)S(1)} %all-to-all-done.1.got_ref, f32[8,12288]{1,0:T(8,128)S(1)} %copy-done.2, f32[8,12288]{1,0:T(8,128)S(1)} %suffix.3.late), custom_call_target="tpu_custom_call" | custom-call | tf_op jit(solution)/shard_map/combine/pallas_call | solution.py:250
  41.2 5.1 %all-to-all-start.2 = ((bf16[8,8,4096]{2,1,0:T(8,128)(2,1)}), bf16[8,8,4096]{2,1,0:T(8,128)(2,1)S(1)}, u32[]{:S(2)}, u32[]{:S(2)}) async-start(bf16[8,8,4096]{2,1,0:T(8,128)(2,1)} %combine.1), calls=%async_computation.2 | async-start | bytes 1048576 | tf_op jit(solution)/shard_map/all_to_all | solution.py:290
  46.2 0.0 collective-permute-done.1.x_ref
  46.2 0.0 copy-start
  46.2 1.3 %copy-done = bf16[4096,256]{1,0:T(8,128)(2,1)} copy-done((bf16[4096,256]{1,0:T(8,128)(2,1)}, bf16[4096,256]{1,0:T(8,128)(2,1)S(1)}, u32[]{:S(2)}) %copy-start) | copy-done | bytes 2097176
  47.6 0.0 copy-start.1
  47.6 1.6 %copy-done.1 = bf16[4096,256]{1,0:T(8,128)(2,1)S(1)} copy-done((bf16[4096,256]{1,0:T(8,128)(2,1)S(1)}, bf16[4096,256]{1,0:T(8,128)(2,1)}, u32[]{:S(2)}) %copy-start.1) | copy-done | bytes 2097176
  49.2 0.1 stage.1
  49.3 4.6 %all-to-all-done.2 = bf16[8,8,4096]{2,1,0:T(8,128)(2,1)S(1)} async-done(((bf16[8,8,4096]{2,1,0:T(8,128)(2,1)}), bf16[8,8,4096]{2,1,0:T(8,128)(2,1)S(1)}, u32[]{:S(2)}, u32[]{:S(2)}) %all-to-all-start.2) | async-done | bytes 524320 | tf_op jit(solution)/shard_map/all_to_all | solution.py:290
  53.9 0.0 copy-start.6
  53.9 0.5 convolution_convert_fusion
  54.4 3.0 %collective-permute-start.2 = (bf16[64,256]{1,0:T(8,128)(2,1)S(1)}, bf16[64,256]{1,0:T(8,128)(2,1)S(1)}, u32[]{:S(2)}, u32[]{:S(2)}) collective-permute-start(bf16[64,256]{1,0:T(8,128)(2,1)S(1)} %convolution_convert_fusion), channel_id=1, source_target_pairs={{0,1},{1,0},{2,3},{3,2},{4,5},{5,4},{6,7},{7,6},{8,9},{9,8},{10,11... | collective-permute-start | bytes 98312 | tf_op jit(solution)/shard_map/ppermute | solution.py:294
  57.4 0.0 copy-done.6
  57.4 0.5 fusion.ours_ref
  57.8 0.4 collective-permute-done.2
  58.2 0.6 %join.1 = bf16[8,16,256]{2,1,0:T(8,128)(2,1)} custom-call(s32[1]{0:T(128)} %bitcast.info, bf16[8,8,256]{2,1,0:T(8,128)(2,1)S(1)} %fusion.ours_ref, bf16[8,8,256]{2,1,0:T(8,128)(2,1)S(1)} %bitcast.32), custom_call_target="tpu_custom_call" | custom-call | tf_op jit(solution)/shard_map/join/pallas_call | solution.py:276
Async XLA Ops:
  0.0 16.9 %collective-permute-start = (bf16[2048,2048]{1,0:T(8,128)(2,1)}, bf16[2048,2048]{1,0:T(8,128)(2,1)}, u32[]{:S(2)}, u32[]{:S(2)}) collective-permute-start(bf16[2048,2048]{1,0:T(8,128)(2,1)} %bitcast.37), channel_id=1, source_target_pairs={{0,1},{1,0},{2,3},{3,2},{4,5},{5,4},{6,7},{7,6},{8,9},{9,8},{10,11... | collective-permute-start | bytes 25165832 | tf_op jit(solution)/shard_map/ppermute | solution.py:294
  0.7 45.6 %collective-permute-start.1 = (bf16[4096,256]{1,0:T(8,128)(2,1)}, bf16[4096,256]{1,0:T(8,128)(2,1)S(1)}, u32[]{:S(2)}, u32[]{:S(2)}) collective-permute-start(bf16[4096,256]{1,0:T(8,128)(2,1)} %param.15), channel_id=1, source_target_pairs={{0,1},{1,0},{2,3},{3,2},{4,5},{5,4},{6,7},{7,6},{8,9},{9,8},{10,11... | collective-permute-start | bytes 6291464 | tf_op jit(solution)/shard_map/ppermute | solution.py:294
  2.4 14.5 %all-to-all-start = ((bf16[8,8,4096]{2,1,0:T(8,128)(2,1)}), bf16[8,8,4096]{2,1,0:T(8,128)(2,1)S(1)}, u32[]{:S(2)}, u32[]{:S(2)}) async-start(bf16[8,8,4096]{2,1,0:T(8,128)(2,1)} %broadcast_in_dim.11), calls=%async_computation | async-start | bytes 1048576 | tf_op jit(solution)/shard_map/all_to_all | solution.py:290
  26.0 14.0 %all-to-all-start.1 = ((bf16[8,8,4352]{2,1,0:T(8,128)(2,1)}), bf16[8,8,4352]{2,1,0:T(8,128)(2,1)S(1)}, u32[]{:S(2)}, u32[]{:S(2)}) async-start(bf16[8,8,4352]{2,1,0:T(8,128)(2,1)} %bitcast.7), calls=%async_computation.1 | async-start | bytes 1114112 | tf_op jit(solution)/shard_map/all_to_all | solution.py:290
  29.6 5.8 %copy-start.3 = (bf16[1,8,4096]{2,1,0:T(8,128)(2,1)S(1)}, bf16[1,8,4096]{2,1,0:T(8,128)(2,1)}, u32[]{:S(2)}) copy-start(bf16[1,8,4096]{2,1,0:T(8,128)(2,1)} %param.8) | copy-start | bytes 196612
  29.6 5.8 %copy-start.4 = (bf16[1,8,2048]{2,1,0:T(8,128)(2,1)S(1)}, bf16[1,8,2048]{2,1,0:T(8,128)(2,1)}, u32[]{:S(2)}) copy-start(bf16[1,8,2048]{2,1,0:T(8,128)(2,1)} %param.14) | copy-start | bytes 98308
  29.6 5.8 %copy-start.5 = (s32[1,8]{1,0:T(1,128)S(1)}, s32[1,8]{1,0:T(1,128)}, u32[]{:S(2)}) copy-start(s32[1,8]{1,0:T(1,128)} %param.13) | copy-start | bytes 100
  35.4 4.6 %copy-start.2 = (f32[8,12288]{1,0:T(8,128)S(1)}, f32[8,12288]{1,0:T(8,128)}, u32[]{:S(2)}) copy-start(f32[8,12288]{1,0:T(8,128)} %suffix.2.early) | copy-start | bytes 1179652
  41.2 12.8 %all-to-all-start.2 = ((bf16[8,8,4096]{2,1,0:T(8,128)(2,1)}), bf16[8,8,4096]{2,1,0:T(8,128)(2,1)S(1)}, u32[]{:S(2)}, u32[]{:S(2)}) async-start(bf16[8,8,4096]{2,1,0:T(8,128)(2,1)} %combine.1), calls=%async_computation.2 | async-start | bytes 1048576 | tf_op jit(solution)/shard_map/all_to_all | solution.py:290
  46.2 1.3 %copy-start = (bf16[4096,256]{1,0:T(8,128)(2,1)}, bf16[4096,256]{1,0:T(8,128)(2,1)S(1)}, u32[]{:S(2)}) copy-start(bf16[4096,256]{1,0:T(8,128)(2,1)S(1)} %collective-permute-done.1.x_ref) | copy-start | bytes 6291460
  47.6 1.6 %copy-start.1 = (bf16[4096,256]{1,0:T(8,128)(2,1)S(1)}, bf16[4096,256]{1,0:T(8,128)(2,1)}, u32[]{:S(2)}) copy-start(bf16[4096,256]{1,0:T(8,128)(2,1)} %copy-done) | copy-start | bytes 6291460
  53.9 3.5 %copy-start.6 = (bf16[4096,256]{1,0:T(8,128)(2,1)S(1)}, bf16[4096,256]{1,0:T(8,128)(2,1)}, u32[]{:S(2)}) copy-start(bf16[4096,256]{1,0:T(8,128)(2,1)} %param.15) | copy-start | bytes 6291460
  54.4 3.8 %collective-permute-start.2 = (bf16[64,256]{1,0:T(8,128)(2,1)S(1)}, bf16[64,256]{1,0:T(8,128)(2,1)S(1)}, u32[]{:S(2)}, u32[]{:S(2)}) collective-permute-start(bf16[64,256]{1,0:T(8,128)(2,1)S(1)} %convolution_convert_fusion), channel_id=1, source_target_pairs={{0,1},{1,0},{2,3},{3,2},{4,5},{5,4},{6,7},{7,6},{8,9},{9,8},{10,11... | collective-permute-start | bytes 98312 | tf_op jit(solution)/shard_map/ppermute | solution.py:294

commit v4 on v3

--- a/solution.py
+++ b/solution.py
@@ -1,5 +1,3 @@
-import functools
-
 import jax
 import jax.numpy as jnp
 from jax import lax
@@ -19,6 +17,7 @@
 LOG2E = 1.4426950408889634
 EXP_SCALE = SCALE * LOG2E
 GROUPS = (1, 3, 8)
+CHIP = ("x", "z")
 STAT = 2 * HD
 
 NT = (((1,), (1,)), ((), ()))
@@ -42,11 +41,12 @@
     return (pltpu.roll(x, HD - 64, 1) + pltpu.roll(x, HD - 32, 1)) + x
 
 
-def prefix_kernel(info, q_ref, own_ref, other_ref, out_ref, cache, even, odd, sems):
+def prefix_kernel(owner, lens, q_ref, own_ref, other_ref, out_ref, cache, even, odd, sems):
     count = q_ref.shape[0]
     positions = cache.shape[0]
-    active = info[0]
-    length = info[2]
+    here = lax.axis_index(CHIP) == lax.div(owner[0], 2)
+    same = lax.axis_index("core") == lax.rem(owner[0], 2)
+    length = lens[0]
     ends = GROUPS
 
     def copies(src):
@@ -62,15 +62,15 @@
         for c in copies(src):
             c.start()
 
-    @pl.when(active == 1)
+    @pl.when(here & same)
     def _():
         start(own_ref)
 
-    @pl.when(active == 2)
+    @pl.when(here & jnp.logical_not(same))
     def _():
         start(other_ref)
 
-    @pl.when(active > 0)
+    @pl.when(here)
     def _():
         waits = copies(own_ref)
         lane = lax.broadcasted_iota(jnp.int32, (count, HD), 1)
@@ -110,15 +110,16 @@
         out_ref[:, QW + HD :] = three_parts(l_all)
 
 
-def prefix_call(info, q, own, other):
+def prefix_call(owner, lens, q, own, other):
     count = q.shape[0]
     positions = own.shape[0]
     vmem = pl.BlockSpec(memory_space=pltpu.VMEM)
     raw = pl.BlockSpec(memory_space=pl.ANY)
+    smem = pl.BlockSpec(memory_space=pltpu.SMEM)
     return pl.pallas_call(
         prefix_kernel,
         out_shape=jax.ShapeDtypeStruct((count, QW + STAT), jnp.bfloat16),
-        in_specs=[pl.BlockSpec(memory_space=pltpu.SMEM), vmem, raw, raw],
+        in_specs=[smem, smem, vmem, raw, raw],
         out_specs=vmem,
         scratch_shapes=[
             pltpu.VMEM((positions, 2 * KW), jnp.bfloat16),
@@ -133,36 +134,33 @@
             transcendentals=count * H * positions,
         ),
         name="prefix",
-    )(info, q, own, other)
-
-
-def suffix_kernel(base, lens, q_ref, new_ref, kv_ref, out_ref, kv, rows, sems):
+    )(owner, lens, q, own, other)
+
+
+def suffix_kernel(lens, q_ref, new_ref, kv_ref, out_ref, kv, rows, sems):
     count, positions = kv.shape[:2]
-    mine = range(base, base + count)
-    copies = {
-        i: pltpu.make_async_copy(kv_ref.at[i], kv.at[i - base], sems.at[i - base]) for i in mine
-    }
-    for i in mine:
-        copies[i].start()
+    copies = [pltpu.make_async_copy(kv_ref.at[i], kv.at[i], sems.at[i]) for i in range(count)]
+    for c in copies:
+        c.start()
     q = q_ref[...].astype(jnp.float32)
     new = new_ref[...].astype(jnp.float32)
     group = lax.broadcasted_iota(jnp.int32, (H, HD), 0) // GRP
     pos = lax.broadcasted_iota(jnp.int32, (1, positions), 1)
-    for i in mine:
+    for i in range(count):
         for h in range(H):
-            rows[i - base, h : h + 1, :] = q[i : i + 1, h * HD : (h + 1) * HD]
-    for i in mine:
-        heads = rows[i - base]
+            rows[i, h : h + 1, :] = q[i : i + 1, h * HD : (h + 1) * HD]
+    for i in range(count):
+        heads = rows[i]
         spread = jnp.concatenate([jnp.where(group == g, heads, 0.0) for g in range(KVH)], axis=1)
         own = jnp.sum(spread * new[i : i + 1, :KW], axis=1, keepdims=True)
         copies[i].wait()
-        s = dot(spread.astype(jnp.bfloat16), kv[i - base, :, :KW], NT)
+        s = dot(spread.astype(jnp.bfloat16), kv[i, :, :KW], NT)
         s = jnp.where(pos < lens[i], s, -1e30)
         top = jnp.maximum(jnp.max(s, axis=1, keepdims=True), own)
         e = jnp.exp2((s - top) * EXP_SCALE)
         own_e = jnp.exp2((own - top) * EXP_SCALE)
         total = jnp.sum(e, axis=1, keepdims=True) + own_e
-        o = dot(e.astype(jnp.bfloat16), kv[i - base, :, KW:], NN)
+        o = dot(e.astype(jnp.bfloat16), kv[i, :, KW:], NN)
         o = o + own_e.astype(jnp.bfloat16).astype(jnp.float32) * new[i : i + 1, KW:]
         picked = o[:, :HD]
         for g in range(1, KVH):
@@ -174,12 +172,12 @@
                 out_ref[i : i + 1, k * QW + h * HD : k * QW + (h + 1) * HD] = part[h : h + 1]
 
 
-def suffix_call(base, count, limit, lens, q, new, kv):
-    samples, positions, width = kv.shape
+def suffix_call(lens, q, new, kv):
+    count, positions, width = kv.shape
     vmem = pl.BlockSpec(memory_space=pltpu.VMEM)
     return pl.pallas_call(
-        functools.partial(suffix_kernel, base),
-        out_shape=jax.ShapeDtypeStruct((samples, 3 * QW), jnp.float32),
+        suffix_kernel,
+        out_shape=jax.ShapeDtypeStruct((count, 3 * QW), jnp.float32),
         in_specs=[
             pl.BlockSpec(memory_space=pltpu.SMEM),
             vmem,
@@ -192,7 +190,7 @@
             pltpu.VMEM((count, H, HD), jnp.float32),
             pltpu.SemaphoreType.DMA((count,)),
         ],
-        compiler_params=pltpu.CompilerParams(vmem_limit_bytes=limit << 20),
+        compiler_params=pltpu.CompilerParams(vmem_limit_bytes=57 << 20),
         cost_estimate=pl.CostEstimate(
             flops=4 * count * H * positions * KW,
             bytes_accessed=4 * count * positions * KW,
@@ -202,33 +200,17 @@
     )(lens, q, new, kv)
 
 
-def stage_kernel(x_ref, out_ref, sem):
-    pltpu.async_copy(x_ref, out_ref, sem).wait()
-
-
-def stage_call(x):
-    return pl.pallas_call(
-        stage_kernel,
-        out_shape=jax.ShapeDtypeStruct(x.shape, x.dtype),
-        in_specs=[pl.BlockSpec(memory_space=pl.ANY)],
-        out_specs=pl.BlockSpec(memory_space=pltpu.VMEM),
-        scratch_shapes=[pltpu.SemaphoreType.DMA],
-        compiler_params=pltpu.CompilerParams(vmem_limit_bytes=4 << 20),
-        cost_estimate=pl.CostEstimate(flops=0, bytes_accessed=2 * x.size, transcendentals=0),
-        name="stage",
-    )(x)
-
-
-def combine_kernel(split, where, got_ref, early, late, out_ref, attn, outs):
-    src = where[0]
+def combine_kernel(owner, got_ref, suf_ref, w_ref, out_ref, w_out, attn, outs, w_sem):
+    load = pltpu.make_async_copy(w_ref, w_out, w_sem)
+    load.start()
+    src = lax.div(owner[0], 2)
     m_pre = from_parts(got_ref[src, :, QW : QW + HD])
     l_pre = from_parts(got_ref[src, :, QW + HD :])
     count = m_pre.shape[0]
-    first = lax.broadcasted_iota(jnp.int32, (count, HD), 0) < split
     for h in range(H):
         at = slice(h * HD, (h + 1) * HD)
         cols = [slice(k * QW + h * HD, k * QW + (h + 1) * HD) for k in range(3)]
-        o_suf, m_suf, l_suf = (jnp.where(first, early[:, c], late[:, c]) for c in cols)
+        o_suf, m_suf, l_suf = (suf_ref[:, c] for c in cols)
         m_h = jnp.broadcast_to(m_pre[:, h : h + 1], (count, HD))
         l_h = jnp.broadcast_to(l_pre[:, h : h + 1], (count, HD))
         top = jnp.maximum(m_h, m_suf)
@@ -242,48 +224,54 @@
         c.start()
     for c in copies:
         c.wait()
-
-
-def combine_call(split, where, got, early, late):
+    load.wait()
+
+
+def combine_call(owner, got, suf, w):
     peers, count, _ = got.shape
     vmem = pl.BlockSpec(memory_space=pltpu.VMEM)
+    raw = pl.BlockSpec(memory_space=pl.ANY)
     return pl.pallas_call(
-        functools.partial(combine_kernel, split),
-        out_shape=jax.ShapeDtypeStruct((peers, count, QW), jnp.bfloat16),
-        in_specs=[pl.BlockSpec(memory_space=pltpu.SMEM), vmem, vmem, vmem],
-        out_specs=pl.BlockSpec(memory_space=pl.ANY),
-        scratch_shapes=[pltpu.VMEM((count, QW), jnp.bfloat16), pltpu.SemaphoreType.DMA((peers,))],
+        combine_kernel,
+        out_shape=[
+            jax.ShapeDtypeStruct((peers, count, QW), jnp.bfloat16),
+            jax.ShapeDtypeStruct(w.shape, w.dtype),
+        ],
+        in_specs=[pl.BlockSpec(memory_space=pltpu.SMEM), vmem, vmem, raw],
+        out_specs=[raw, vmem],
+        scratch_shapes=[
+            pltpu.VMEM((count, QW), jnp.bfloat16),
+            pltpu.SemaphoreType.DMA((peers,)),
+            pltpu.SemaphoreType.DMA,
+        ],
         compiler_params=pltpu.CompilerParams(vmem_limit_bytes=8 << 20),
         name="combine",
-    )(where, got, early, late)
+    )(owner, got, suf, w)
 
 
 def project(x, w):
     return jnp.dot(x, w, preferred_element_type=jnp.float32).astype(jnp.bfloat16)
 
 
-def join_kernel(info, ours_ref, back_ref, out_ref):
+def join_kernel(ours_ref, back_ref, out_ref):
     count = ours_ref.shape[1]
     ours, back = ours_ref[...], back_ref[...]
-    first = info[0] == 0
+    first = lax.axis_index("core") == 0
     out_ref[:, :count] = jnp.where(first, ours, back)
     out_ref[:, count:] = jnp.where(first, back, ours)
 
 
-def join_call(core, ours, back):
+def join_call(ours, back):
     peers, count, cols = ours.shape
     vmem = pl.BlockSpec(memory_space=pltpu.VMEM)
     return pl.pallas_call(
         join_kernel,
         out_shape=jax.ShapeDtypeStruct((peers, 2 * count, cols), ours.dtype),
-        in_specs=[pl.BlockSpec(memory_space=pltpu.SMEM), vmem, vmem],
+        in_specs=[vmem, vmem],
         out_specs=vmem,
         compiler_params=pltpu.CompilerParams(vmem_limit_bytes=4 << 20),
         name="join",
-    )(core, ours, back)
-
-
-CHIP = ("x", "z")
+    )(ours, back)
 
 
 def to_chips(x):
@@ -296,31 +284,21 @@
 
 def local(queries, prompt_cache, owner, prompt_len, suffix_cache, suffix_len, new_kv, out_weight):
     peers = lax.axis_size(CHIP)
-    core = lax.axis_index("core")
     q = queries[0]
     count = q.shape[0]
-    split = 4
     own_cache = prompt_cache[0, 0]
-    chip = owner[0] // 2
-    mine = lax.axis_index(CHIP) == chip
-    active = jnp.where(mine, jnp.where(owner[0] % 2 == core, 1, 2), 0)
-    info = jnp.stack([active, chip, prompt_len[0]]).astype(jnp.int32)
-    suffix_args = (suffix_len[0], q, new_kv[0], suffix_cache[0])
     other_cache = partner(own_cache)
-    q_copies = jnp.broadcast_to(q, (peers, *q.shape))
-    all_q = to_chips(q_copies).reshape(peers * count, QW)
-    early = suffix_call(0, split, 57, *suffix_args)
-    sent = prefix_call(info, all_q, own_cache, other_cache)
+    all_q = to_chips(jnp.broadcast_to(q, (peers, *q.shape))).reshape(peers * count, QW)
+    sent = prefix_call(owner, prompt_len, all_q, own_cache, other_cache)
     got = to_chips(sent.reshape(peers, count, QW + STAT))
-    late = suffix_call(split, count - split, 50, *suffix_args)
-    attn = combine_call(split, chip[None], got, early, late)
+    suf = suffix_call(suffix_len[0], q, new_kv[0], suffix_cache[0])
+    other_weight = partner(out_weight)
+    attn, other_weight = combine_call(owner, got, suf, other_weight)
     attn = to_chips(attn).reshape(peers * count, QW)
-    other_weight = partner(out_weight)
-    other_weight = stage_call(other_weight)
     theirs = project(attn, other_weight)
     back = partner(theirs).reshape(peers, count, -1)
     ours = project(attn, out_weight).reshape(peers, count, -1)
-    mixed = join_call(core[None], ours, back)
+    mixed = join_call(ours, back)
     return mixed.reshape(1, 2 * peers * count, -1)
 
 

time: 59.4 us -> 57.9 us (0.975)
  the two profiles are of different devices: /device:TPU:9 before, /device:TPU:17 now
where the time goes in v4:
time: 57.9 us; the launch traced here: 57.4 us
  Pallas kernels  18.9 us (33%)
  starting transfers between devices  12.9 us (22%)
  blocking collectives  12.2 us (21%)
  waiting for transfers between devices  8.47 us (15%)
  local copies, waits for them, and re-layouts  2.72 us (5%)
  between operations  1.36 us (2%)
  matrix products  0.93 us (2%)
    all_to_all x1, blocking collectives, to_chips(): return lax.all_to_all(x, CHIP, split_axis=0, concat_axis=0, tiled=True)  12.2 us
    all_to_all x2, starting transfers between devices, to_chips(): return lax.all_to_all(x, CHIP, split_axis=0, concat_axis=0, tiled=True)  8.92 us
    pallas_call x1, Pallas kernels, prefix_call(): pl.pallas_call(prefix_kernel, out_shape=jax.ShapeDtypeStruct((count, QW +...  8.59 us
    pallas_call x1, Pallas kernels, suffix_call(): pl.pallas_call(suffix_kernel, out_shape=jax.ShapeDtypeStruct((count, 3 *...  8.49 us
    all_to_all x2, waiting for transfers between devices, to_chips(): return lax.all_to_all(x, CHIP, split_axis=0, concat_axis=0, tiled=True)  8.07 us
    ppermute x3, starting transfers between devices, partner(): return lax.ppermute(x, 'core', [(0, 1), (1, 0)])  3.99 us
    broadcast_in_dim x1, local copies, waits for them, and re-layouts, local(): jnp.broadcast_to(q, (peers, *q.shape))  1.72 us
    pallas_call x1, Pallas kernels, combine_call(): pl.pallas_call(combine_kernel, out_shape=[jax.ShapeDtypeStruct((peers, co...  1.17 us
  transfers between devices with their start and end apart: 5, of which 3 were waited for; matrix products, arithmetic and copies ran while one was open for 4% of the time, Pallas kernels for 30%

profile of v4, /device:TPU:17, one launch (start us, length us, event | category | flops | bytes accessed | tf_op | source)
XLA Modules:
  0.0 57.4 jit_solution(11774717494675788285)
XLA Ops:
  0.0 0.7 %collective-permute-start = (bf16[2048,2048]{1,0:T(8,128)(2,1)}, bf16[2048,2048]{1,0:T(8,128)(2,1)}, u32[]{:S(2)}, u32[]{:S(2)}) collective-permute-start(bf16[2048,2048]{1,0:T(8,128)(2,1)} %bitcast.20), channel_id=1, source_target_pairs={{0,1},{1,0},{2,3},{3,2},{4,5},{5,4},{6,7},{7,6},{8,9},{9,8},{10,11... | collective-permute-start | bytes 25165832 | tf_op jit(solution)/shard_map/ppermute | solution.py:282
  0.7 0.0 collective-permute-start.1
  0.7 1.7 %broadcast_in_dim.3 = bf16[8,8,4096]{2,1,0:T(8,128)(2,1)} broadcast(bf16[8,4096]{1,0:T(8,128)(2,1)} %bitcast.23), dimensions={1,2} | broadcast | bytes 589824 | tf_op jit(solution)/shard_map/broadcast_in_dim | solution.py:291
  2.4 5.4 %all-to-all-start = ((bf16[8,8,4096]{2,1,0:T(8,128)(2,1)}), bf16[8,8,4096]{2,1,0:T(8,128)(2,1)S(1)}, u32[]{:S(2)}, u32[]{:S(2)}) async-start(bf16[8,8,4096]{2,1,0:T(8,128)(2,1)} %broadcast_in_dim.3), calls=%async_computation | async-start | bytes 1048576 | tf_op jit(solution)/shard_map/all_to_all | solution.py:278
  9.1 7.8 %all-to-all-done = bf16[8,8,4096]{2,1,0:T(8,128)(2,1)S(1)} async-done(((bf16[8,8,4096]{2,1,0:T(8,128)(2,1)}), bf16[8,8,4096]{2,1,0:T(8,128)(2,1)S(1)}, u32[]{:S(2)}, u32[]{:S(2)}) %all-to-all-start) | async-done | bytes 524320 | tf_op jit(solution)/shard_map/all_to_all | solution.py:278
  16.9 0.0 collective-permute-done.other_ref
  16.9 8.6 %prefix.1 = bf16[64,4352]{1,0:T(8,128)(2,1)} custom-call(s32[1]{0:T(128)S(6)} %copy.9.owner, s32[1]{0:T(128)S(6)} %copy.10.lens, bf16[64,4096]{1,0:T(8,128)(2,1)S(1)} %bitcast.18, bf16[2048,2048]{1,0:T(8,128)(2,1)} %bitcast.21, bf16[2048,2048]{1,0:T(8,128)(2,1)} %collective-permute-done.other_ref), custom_call_target="tpu_custom_call" | custom-call | flops 2147483648 | bytes 8388608 | tf_op jit(solution)/shard_map/prefix/pallas_call | solution.py:119
  25.5 3.5 %all-to-all-start.1 = ((bf16[8,8,4352]{2,1,0:T(8,128)(2,1)}), bf16[8,8,4352]{2,1,0:T(8,128)(2,1)S(1)}, u32[]{:S(2)}, u32[]{:S(2)}) async-start(bf16[8,8,4352]{2,1,0:T(8,128)(2,1)} %bitcast.3), calls=%async_computation.1 | async-start | bytes 1114112 | tf_op jit(solution)/shard_map/all_to_all | solution.py:278
  29.0 8.5 %suffix.1.suf_ref = f32[8,12288]{1,0:T(8,128)} custom-call(s32[8]{0:T(128)} %bitcast.26, bf16[8,4096]{1,0:T(8,128)(2,1)} %bitcast.24, bf16[8,2048]{1,0:T(8,128)(2,1)} %bitcast.25, bf16[8,256,2048]{2,1,0:T(8,128)(2,1)} %bitcast.22), custom_call_target="tpu_custom_call" | custom-call | flops 268435456 | bytes 8388608 | tf_op jit(solution)/shard_map/suffix/pallas_call | solution.py:178
  37.5 0.0 collective-permute-done.1.w_ref
  37.5 0.3 all-to-all-done.1.got_ref
  37.8 0.0 copy-start
  37.8 1.0 %copy-done = f32[8,12288]{1,0:T(8,128)S(1)} copy-done((f32[8,12288]{1,0:T(8,128)S(1)}, f32[8,12288]{1,0:T(8,128)}, u32[]{:S(2)}) %copy-start) | copy-done | bytes 393240
  38.8 1.2 %combine.1 = (bf16[8,8,4096]{2,1,0:T(8,128)(2,1)S(1)}, bf16[4096,256]{1,0:T(8,128)(2,1)S(1)}) custom-call(s32[1]{0:T(128)S(6)} %copy.9.owner, bf16[8,8,4352]{2,1,0:T(8,128)(2,1)S(1)} %all-to-all-done.1.got_ref, f32[8,12288]{1,0:T(8,128)S(1)} %copy-done, bf16[4096,256]{1,0:T(8,128)(2,1)S(1)} %collective-permute-done.1.w_ref), custom_call_target="tpu_custom_call" | custom-call | tf_op jit(solution)/shard_map/combine/pallas_call | solution.py:234
  40.0 0.0 copy-start.1
  40.0 12.2 %all_to_all.15 = bf16[8,8,4096]{2,1,0:T(8,128)(2,1)S(1)} all-to-all(bf16[8,8,4096]{2,1,0:T(8,128)(2,1)S(1)} %get-tuple-element.7), channel_id=1, replica_groups=mesh['prompt'=8,'x'=4,'z'=2,'core'=2] {'x','z'}, dimensions={0} | all-to-all | bytes 1048576 | tf_op jit(solution)/shard_map/all_to_all | solution.py:278
  52.2 0.5 convolution_convert_fusion
  52.6 3.3 %collective-permute-start.2 = (bf16[64,256]{1,0:T(8,128)(2,1)S(1)}, bf16[64,256]{1,0:T(8,128)(2,1)S(1)}, u32[]{:S(2)}, u32[]{:S(2)}) collective-permute-start(bf16[64,256]{1,0:T(8,128)(2,1)S(1)} %convolution_convert_fusion), channel_id=1, source_target_pairs={{0,1},{1,0},{2,3},{3,2},{4,5},{5,4},{6,7},{7,6},{8,9},{9,8},{10,11... | collective-permute-start | bytes 98312 | tf_op jit(solution)/shard_map/ppermute | solution.py:282
  55.9 0.0 copy-done.1
  55.9 0.5 fusion.ours_ref
  56.4 0.4 collective-permute-done.2
  56.8 0.6 %join.1 = bf16[8,16,256]{2,1,0:T(8,128)(2,1)} custom-call(bf16[8,8,256]{2,1,0:T(8,128)(2,1)S(1)} %fusion.ours_ref, bf16[8,8,256]{2,1,0:T(8,128)(2,1)S(1)} %bitcast.19), custom_call_target="tpu_custom_call" | custom-call | tf_op jit(solution)/shard_map/join/pallas_call | solution.py:267
Async XLA Ops:
  0.0 16.9 %collective-permute-start = (bf16[2048,2048]{1,0:T(8,128)(2,1)}, bf16[2048,2048]{1,0:T(8,128)(2,1)}, u32[]{:S(2)}, u32[]{:S(2)}) collective-permute-start(bf16[2048,2048]{1,0:T(8,128)(2,1)} %bitcast.20), channel_id=1, source_target_pairs={{0,1},{1,0},{2,3},{3,2},{4,5},{5,4},{6,7},{7,6},{8,9},{9,8},{10,11... | collective-permute-start | bytes 25165832 | tf_op jit(solution)/shard_map/ppermute | solution.py:282
  0.7 36.8 %collective-permute-start.1 = (bf16[4096,256]{1,0:T(8,128)(2,1)}, bf16[4096,256]{1,0:T(8,128)(2,1)S(1)}, u32[]{:S(2)}, u32[]{:S(2)}) collective-permute-start(bf16[4096,256]{1,0:T(8,128)(2,1)} %param.15), channel_id=1, source_target_pairs={{0,1},{1,0},{2,3},{3,2},{4,5},{5,4},{6,7},{7,6},{8,9},{9,8},{10,11... | collective-permute-start | bytes 6291464 | tf_op jit(solution)/shard_map/ppermute | solution.py:282
  2.4 14.5 %all-to-all-start = ((bf16[8,8,4096]{2,1,0:T(8,128)(2,1)}), bf16[8,8,4096]{2,1,0:T(8,128)(2,1)S(1)}, u32[]{:S(2)}, u32[]{:S(2)}) async-start(bf16[8,8,4096]{2,1,0:T(8,128)(2,1)} %broadcast_in_dim.3), calls=%async_computation | async-start | bytes 1048576 | tf_op jit(solution)/shard_map/all_to_all | solution.py:278
  25.5 12.3 %all-to-all-start.1 = ((bf16[8,8,4352]{2,1,0:T(8,128)(2,1)}), bf16[8,8,4352]{2,1,0:T(8,128)(2,1)S(1)}, u32[]{:S(2)}, u32[]{:S(2)}) async-start(bf16[8,8,4352]{2,1,0:T(8,128)(2,1)} %bitcast.3), calls=%async_computation.1 | async-start | bytes 1114112 | tf_op jit(solution)/shard_map/all_to_all | solution.py:278
  37.8 1.0 %copy-start = (f32[8,12288]{1,0:T(8,128)S(1)}, f32[8,12288]{1,0:T(8,128)}, u32[]{:S(2)}) copy-start(f32[8,12288]{1,0:T(8,128)} %suffix.1.suf_ref) | copy-start | bytes 1179652
  40.0 16.0 %copy-start.1 = (bf16[4096,256]{1,0:T(8,128)(2,1)S(1)}, bf16[4096,256]{1,0:T(8,128)(2,1)}, u32[]{:S(2)}) copy-start(bf16[4096,256]{1,0:T(8,128)(2,1)} %param.15) | copy-start | bytes 6291460
  52.6 4.2 %collective-permute-start.2 = (bf16[64,256]{1,0:T(8,128)(2,1)S(1)}, bf16[64,256]{1,0:T(8,128)(2,1)S(1)}, u32[]{:S(2)}, u32[]{:S(2)}) collective-permute-start(bf16[64,256]{1,0:T(8,128)(2,1)S(1)} %convolution_convert_fusion), channel_id=1, source_target_pairs={{0,1},{1,0},{2,3},{3,2},{4,5},{5,4},{6,7},{7,6},{8,9},{9,8},{10,11... | collective-permute-start | bytes 98312 | tf_op jit(solution)/shard_map/ppermute | solution.py:282
